TPU v7x, 32 devices: a whole 2x2x4 slice. The times are simulated.
32 devices in a mesh: row: 8 (over z, x), col: 4 (over y, core).
Axes of the slice: x: 2, y: 2, z: 4, core: 2. Of those that a mesh axis runs over, the one named last changes fastest.
Arguments:
- mom_a: float32 [1536, 12288], P('row', 'col'), may hold values from -6 to 6
- grad_a: float32 [1536, 12288], P('row', 'col'), may hold values from -6 to 6
- basis_a: float32 [512, 12288], P('row', 'col'), may hold values from -0.0546875 to 0.0546875
- mom_b: float32 [7168, 1536], P('row', 'col'), may hold values from -6 to 6
- grad_b: float32 [7168, 1536], P('row', 'col'), may hold values from -6 to 6
- basis_b: float32 [512, 1536], P('row', 'col'), may hold values from -0.15625 to 0.15625
Outputs:
- new_mom_a: float32 [1536, 12288], P('row', 'col')
- update_a: bfloat16 [1536, 12288], P('row', 'col')
- new_basis_a: float32 [512, 12288], P('row', 'col')
- new_mom_b: float32 [7168, 1536], P('row', 'col')
- update_b: bfloat16 [7168, 1536], P('row', 'col')
- new_basis_b: float32 [512, 1536], P('row', 'col')
All inputs are finite; a program needn't handle non-finite values.
Results may differ from a plain program's by a relative error of at most 0.0049.
Values sent between devices are 32-bit elements; how exact they have to be, the bound alone decides.
A program may use at most 128 MiB of HBM per device.

v0:
```python
import functools
import math

import jax
import jax.numpy as jnp
from jax import lax
from jax.experimental import pallas as pl
from jax.experimental.pallas import tpu as pltpu
from jax.sharding import PartitionSpec as P

MU = 0.95
EPS = 1e-06
BLOCK = 128
HIGHEST = lax.Precision.HIGHEST


def dot(x, y, contract=((1,), (0,))):
    return lax.dot_general(
        x, y, (contract, ((), ())), precision=HIGHEST, preferred_element_type=jnp.float32
    )


def inverse_kernel(rank, *refs):
    count = len(refs) // 4
    grams, outs = refs[:count], refs[count : 2 * count]
    works, diags = refs[2 * count : 3 * count], refs[3 * count :]
    eye_rows = lax.broadcasted_iota(jnp.int32, (rank, rank), 0)
    eye_cols = lax.broadcasted_iota(jnp.int32, (rank, rank), 1)
    for gram, work in zip(grams, works):
        work[:, :rank] = gram[...]
        work[:, rank:] = (eye_rows == eye_cols).astype(jnp.float32)
    rows = lax.broadcasted_iota(jnp.int32, (BLOCK, 1), 0)
    lanes = lax.broadcasted_iota(jnp.int32, (1, BLOCK), 1)
    for k in range(rank // BLOCK):
        low, high = k * BLOCK, (k + 1) * BLOCK
        for work, diag in zip(works, diags):
            diag[:, :BLOCK] = work[low:high, low:high]
            diag[:, BLOCK:] = (rows == lanes).astype(jnp.float32)

        def step(j, carry):
            for diag in diags:
                here = lanes == j
                row = diag[pl.ds(j, 1), :]
                col = jnp.sum(jnp.where(here, diag[:, :BLOCK], 0.0), axis=1, keepdims=True)
                pivot = jnp.sum(jnp.where(here, row[:, :BLOCK], 0.0), axis=1, keepdims=True)
                factor = jnp.where(rows > j, col * (1.0 / pivot), 0.0)
                diag[...] = diag[...] - factor * row
            return carry

        lax.fori_loop(0, BLOCK, step, 0)
        width = slice(low, rank + high)
        for work, diag in zip(works, diags):
            pivots = jnp.sum(
                jnp.where(rows == lanes, diag[:, :BLOCK], 0.0), axis=1, keepdims=True
            )
            inverse = diag[:, BLOCK:] * (1.0 / jnp.sqrt(pivots))
            panel = dot(inverse, work[low:high, width])
            work[low:high, width] = panel
            if high < rank:
                factors = panel[:, BLOCK : rank - low]
                work[high:, width] = work[high:, width] - dot(factors, panel, ((0,), (0,)))
    for work, out in zip(works, outs):
        out[...] = work[:, rank:]


def inverse_factors(*grams):
    rank = grams[0].shape[0]
    count = len(grams)
    return pl.pallas_call(
        functools.partial(inverse_kernel, rank),
        out_shape=[jax.ShapeDtypeStruct((rank, rank), jnp.float32)] * count,
        in_specs=[pl.BlockSpec(memory_space=pltpu.VMEM)] * count,
        out_specs=[pl.BlockSpec(memory_space=pltpu.VMEM)] * count,
        scratch_shapes=[pltpu.VMEM((rank, 2 * rank), jnp.float32)] * count
        + [pltpu.VMEM((BLOCK, 2 * BLOCK), jnp.float32)] * count,
        compiler_params=pltpu.CompilerParams(vmem_limit_bytes=24 * 1024 * 1024),
    )(*grams)


def reduce_rows(partial_sum):
    share_count = lax.axis_size("row")
    shares = partial_sum.reshape(share_count, -1, partial_sum.shape[1])
    return jnp.sum(lax.all_to_all(shares, "row", 0, 0), axis=0)


def shards(mom_a, grad_a, basis_a, mom_b, grad_b, basis_b):
    row_count, col_count = lax.axis_size("row"), lax.axis_size("col")
    buffer_a, buffer_b = MU * mom_a + grad_a, MU * mom_b + grad_b
    last = ((1,), (1,))
    first = ((0,), (0,))
    both = lax.all_gather(jnp.concatenate([basis_a, basis_b], axis=1), "row", axis=0, tiled=True)
    full_a, full_b = both[:, : buffer_a.shape[1]], both[:, buffer_a.shape[1] :]
    partial_a, partial_b, held_a = lax.optimization_barrier(
        (dot(buffer_a, full_a, last), dot(buffer_b, full_b, last), buffer_a)
    )
    proj_a, proj_b = lax.psum((partial_a, partial_b), "col")
    tall_a = lax.all_to_all(held_a, "row", 1, 0, tiled=True)
    proj_a, proj_b, tall_a = lax.optimization_barrier((proj_a, proj_b, tall_a))
    rank = proj_a.shape[1]
    share = rank // row_count

    shares_b = reduce_rows(
        jnp.concatenate([dot(proj_b, proj_b, first), dot(proj_b, buffer_b, first)], axis=1)
    )
    share_b = shares_b[:, rank:]
    gathered = lax.all_gather(jnp.concatenate([proj_a, shares_b[:, :rank]]), "row", axis=0)
    proj_rows = proj_a.shape[0]
    all_a = gathered[:, :proj_rows].reshape(-1, rank)
    gram_b = gathered[:, proj_rows:].reshape(rank, rank)
    gram_a = dot(all_a, all_a, first)
    block_a = dot(all_a, tall_a, first)
    inverse_a, inverse_b = inverse_factors(gram_a, gram_b)

    width_a, width_b = block_a.shape[1], share_b.shape[1]
    width = max(width_a, width_b)
    products = lax.all_gather(
        jnp.concatenate(
            [
                jnp.pad(block_a, ((0, 0), (0, width - width_a))),
                jnp.pad(share_b, ((0, 0), (0, width - width_b))),
            ]
        ),
        "row",
        axis=1,
        tiled=True,
    )
    product_a = products[:rank]
    product_b = products[rank:].reshape(share, row_count, width).swapaxes(0, 1)
    product_b = product_b.reshape(rank, width)[:, :width_b]
    if width != width_a:
        product_a = product_a.reshape(rank, row_count, width)[:, :, :width_a].reshape(rank, -1)

    ortho_a, ortho_b = dot(proj_a, inverse_a, last), dot(proj_b, inverse_b, last)
    trans_a, trans_b = dot(inverse_a, product_a), dot(inverse_b, product_b)
    squares_a, squares_b = lax.psum(
        (
            jnp.sum(trans_a * trans_a, axis=1, keepdims=True),
            jnp.sum(trans_b * trans_b, axis=1, keepdims=True),
        ),
        "col",
    )
    start = lax.axis_index("row") * share
    first_out = finish(buffer_a, ortho_a, trans_a, squares_a, start, share)
    second_out = finish(buffer_b, ortho_b, trans_b, squares_b, start, share)
    return (*first_out, *second_out)


def finish(buffer, ortho, trans, squares, start, share):
    rank = ortho.shape[1]
    total_rows = buffer.shape[0] * lax.axis_size("row")
    total_cols = buffer.shape[1] * lax.axis_size("col")
    full_basis = trans / jnp.sqrt(squares + EPS)
    own_basis = lax.dynamic_slice_in_dim(full_basis, start, share, 0)
    new_mom = buffer - (1.0 - MU) * dot(ortho, trans)
    update = dot(ortho, full_basis) * math.sqrt(total_rows * total_cols / rank)
    return new_mom, update.astype(jnp.bfloat16), own_basis


def solution(mesh):
    spec = P("row", "col")
    return jax.shard_map(
        shards, mesh=mesh, in_specs=(spec,) * 6, out_specs=(spec,) * 6, check_vma=False
    )
```

profile of v0, /device:TPU:0, one launch (start us, length us, event | category | flops | bytes accessed | tf_op | source)
XLA Modules:
  0.0 504.4 jit_solution(2117930563538719035)
XLA Ops:
  9.4 2.7 multiply_add_fusion
  12.1 109.7 %all-gather.5.cloned.1.call-done = f32[512,3456]{1,0:T(8,128)} async-done(((f32[64,3456]{1,0:T(8,128)}), f32[512,3456]{1,0:T(8,128)}) %all-gather.5.cloned.1.call-update) | async-done | bytes 7077904 | tf_op jit(solution)/shard_map/all_gather | solution.py:91
  121.8 9.3 %fusion.2 = f32[192,512]{1,0:T(8,128)} fusion(f32[192,3072]{1,0:T(8,128)S(1)} %multiply_add_fusion, f32[512,3456]{1,0:T(8,128)} %all-gather.5.cloned.1.call-done), kind=kOutput, calls=%fused_computation.2 | convolution fusion | flops 3623878656 | bytes 9043968 | tf_op jit(solution)/shard_map/dot_general | solution.py:18
  131.1 5.5 %fusion.8 = f32[896,512]{1,0:T(8,128)} fusion(f32[512,3456]{1,0:T(8,128)} %all-gather.5.cloned.1.call-done, f32[896,384]{1,0:T(8,128)S(1)} %copy-done.6, f32[896,384]{1,0:T(8,128)S(1)} %copy-done.8), kind=kOutput, calls=%fused_computation.22 | convolution fusion | flops 2114617344 | bytes 5373952 | tf_op jit(solution)/shard_map/dot_general | solution.py:18
  138.2 4.5 all-to-all-start
  143.7 57.7 %all-reduce.4.cloned.1.call-done = (f32[192,512]{1,0:T(8,128)}, f32[896,512]{1,0:T(8,128)}) async-done(((f32[192,512]{1,0:T(8,128)}, f32[896,512]{1,0:T(8,128)}), (f32[192,512]{1,0:T(8,128)}, f32[896,512]{1,0:T(8,128)})) %all-reduce.4.cloned.1.call-update) | async-done | bytes 2228240 | tf_op jit(solution)/shard_map/psum | solution.py:96
  201.4 4.4 fusion.11
  205.8 3.6 fusion.12
  211.2 48.0 %all_to_all.24 = f32[8,64,896]{2,1,0:T(8,128)S(1)} all-to-all(f32[8,64,896]{2,1,0:T(8,128)} %bitcast.49), channel_id=1, replica_groups=mesh['row'=8,'col'=4] {'row'}, dimensions={0} | all-to-all | bytes 3670016 | tf_op jit(solution)/shard_map/all_to_all | solution.py:83
  261.7 70.7 %all-gather.9.cloned.1.call-done = f32[2048,512]{1,0:T(8,128)} async-done(((f32[256,512]{1,0:T(8,128)}), f32[2048,512]{1,0:T(8,128)}) %all-gather.9.cloned.1.call-update) | async-done | bytes 4194320 | tf_op jit(solution)/shard_map/all_gather | solution.py:106
  332.4 2.2 slice.35
  334.6 6.9 %fusion.14 = f32[512,384]{1,0:T(8,128)S(1)} fusion(f32[1536,512]{1,0:T(8,128)S(1)} %bitcast.47, f32[1536,384]{1,0:T(8,128)} %bitcast.1), kind=kOutput, calls=%fused_computation.35 | convolution fusion | flops 3623878656 | bytes 6291456 | tf_op jit(solution)/shard_map/dot_general | solution.py:18
  343.9 8.0 %convolution_bitcast_fusion.refs_0_ = f32[512,512]{1,0:T(8,128)S(1)} fusion(f32[8,256,512]{2,1,0:T(8,128)} %bitcast.53), kind=kOutput, calls=%fused_computation.17 | convolution fusion | flops 4831838208 | bytes 4194304 | tf_op jit(solution)/shard_map/dot_general | solution.py:18
  351.9 68.2 %shard_map.109 = (f32[512,512]{1,0:T(8,128)S(1)}, f32[512,512]{1,0:T(8,128)S(1)}) custom-call(f32[512,512]{1,0:T(8,128)S(1)} %convolution_bitcast_fusion.refs_0_, f32[512,512]{1,0:T(8,128)S(1)} %bitcast.45), custom_call_target="tpu_custom_call" | custom-call | tf_op jit(solution)/shard_map/pallas_call | solution.py:69
  422.0 4.4 fusion.15
  426.3 23.2 %all-gather.7.cloned.1.call-done = f32[576,3072]{1,0:T(8,128)} async-done(((f32[576,384]{1,0:T(8,128)}), f32[576,3072]{1,0:T(8,128)}) %all-gather.7.cloned.1.call-update) | async-done | bytes 7077904 | tf_op jit(solution)/shard_map/all_gather | solution.py:116
  450.7 2.7 multiply_reduce_fusion.1
  453.4 12.8 %multiply_reduce_fusion = (f32[512]{0:T(512)S(1)}, f32[512,3072]{1,0:T(8,128)S(1)}) fusion(f32[512,512]{1,0:T(8,128)S(1)} %get-tuple-element.19, f32[576,3072]{1,0:T(8,128)} %all-gather.7.cloned.1.call-done), kind=kOutput, calls=%fused_computation.4 | convolution fusion | flops 9666822144 | bytes 13633536 | tf_op jit(solution)/shard_map/dot_general | solution.py:18
  466.3 5.8 %fusion.4 = f32[192,3072]{1,0:T(8,128)} fusion(f32[192,3072]{1,0:T(8,128)S(1)} %copy-done.2, f32[192,512]{1,0:T(8,128)S(1)} %copy-done.12, f32[512,3072]{1,0:T(8,128)S(1)} %get-tuple-element.27), kind=kOutput, calls=%fused_computation.7 | convolution fusion | flops 3625058304 | bytes 11403264 | tf_op jit(solution)/shard_map/dot_general | solution.py:18
  472.1 5.9 %all-reduce = (f32[512,1]{0,1:T(1,128)S(1)}, f32[512,1]{0,1:T(1,128)S(1)}) all-reduce(f32[512,1]{0,1:T(1,128)S(1)} %bitcast.55, f32[512,1]{0,1:T(1,128)S(1)} %bitcast.57), channel_id=1, replica_groups=mesh['row'=8,'col'=4] {'col'}, use_global_device_ids=true, to_apply=%region_4.5 | all-reduce | flops 1024 | bytes 8192 | tf_op jit(solution)/shard_map/psum | solution.py:135
  478.0 3.6 broadcast_divide_fusion
  481.6 5.4 %fusion.5 = bf16[192,3072]{1,0:T(8,128)(2,1)} fusion(f32[192,512]{1,0:T(8,128)S(1)} %copy-done.12, f32[512,3072]{1,0:T(8,128)S(1)} %broadcast_divide_fusion), kind=kOutput, calls=%fused_computation.8 | convolution fusion | flops 3625058304 | bytes 7864320 | tf_op jit(solution)/shard_map/dot_general | solution.py:18
  488.7 4.1 fusion.6
  492.9 3.9 fusion.7
  (58 shorter events, 17.0 us)
Async XLA Ops:
  7.2 114.6 %all-gather.5.cloned.1.call-start = ((), (), s32[]{:S(2)}) async-start(), calls=%async_computation.2 | async-start | bytes 7962624 | tf_op jit(solution)/shard_map/all_gather | solution.py:91
  12.1 124.5 %copy-start.1 = (f32[192,3072]{1,0:T(8,128)}, f32[192,3072]{1,0:T(8,128)S(1)}, u32[]{:S(2)}) copy-start(f32[192,3072]{1,0:T(8,128)S(1)} %multiply_add_fusion) | copy-start | bytes 7077892
  121.8 9.3 %copy-start.6 = (f32[896,384]{1,0:T(8,128)S(1)}, f32[896,384]{1,0:T(8,128)}, u32[]{:S(2)}) copy-start(f32[896,384]{1,0:T(8,128)} %param.10) | copy-start | bytes 4128772
  121.8 9.3 %copy-start.8 = (f32[896,384]{1,0:T(8,128)S(1)}, f32[896,384]{1,0:T(8,128)}, u32[]{:S(2)}) copy-start(f32[896,384]{1,0:T(8,128)} %param.9) | copy-start | bytes 4128772
  138.2 63.2 %copy-start.9 = (f32[896,384]{1,0:T(8,128)S(1)}, f32[896,384]{1,0:T(8,128)}, u32[]{:S(2)}) copy-start(f32[896,384]{1,0:T(8,128)} %param.9) | copy-start | bytes 4128772
  138.2 63.2 %all-to-all-start = ((f32[192,8,384]{2,0,1:T(8,128)}), f32[192,8,384]{2,0,1:T(8,128)}, u32[]{:S(2)}, u32[]{:S(2)}) async-start(f32[192,8,384]{2,0,1:T(8,128)} %bitcast.48), calls=%async_computation | async-start | bytes 4718592 | tf_op jit(solution)/shard_map/all_to_all | solution.py:97
  142.7 58.7 %copy-start.7 = (f32[896,384]{1,0:T(8,128)S(1)}, f32[896,384]{1,0:T(8,128)}, u32[]{:S(2)}) copy-start(f32[896,384]{1,0:T(8,128)} %param.10) | copy-start | bytes 4128772
  142.7 58.7 %all-reduce.4.cloned.1.call-start = ((), (), s32[]{:S(2)}) async-start(), calls=%async_computation.5 | async-start | bytes 4456448 | tf_op jit(solution)/shard_map/psum | solution.py:96
  143.4 188.9 %all-gather.9.cloned.1.call-start = ((), (), s32[]{:S(2)}) async-start(), calls=%async_computation.4 | async-start | bytes 4718592 | tf_op jit(solution)/shard_map/all_gather | solution.py:106
  201.3 4.4 copy-start.3
  259.3 75.3 %copy-start.14 = (f32[64,896]{1,0:T(8,128)}, f32[64,896]{1,0:T(8,128)S(1)}, u32[]{:S(2)}) copy-start(f32[64,896]{1,0:T(8,128)S(1)} %reduce_sum.27) | copy-start | bytes 688132
  261.2 188.3 %all-gather.7.cloned.1.call-start = ((), (), s32[]{:S(2)}) async-start(), calls=%async_computation.3 | async-start | bytes 7962624 | tf_op jit(solution)/shard_map/all_gather | solution.py:116
  334.6 7.0 %slice-start.1 = ((f32[64,896]{1,0:T(8,128)}), f32[64,384]{1,0:T(8,128)S(1)}, s32[]{:S(2)}) async-start(f32[64,896]{1,0:T(8,128)} %copy-done.14), calls=%async_computation.7 | async-start | bytes 196608 | tf_op jit(solution)/shard_map/slice | solution.py:105
  351.8 68.2 %copy-start.13 = (f32[192,512]{1,0:T(8,128)S(1)}, f32[192,512]{1,0:T(8,128)}, u32[]{:S(2)}) copy-start(f32[192,512]{1,0:T(8,128)} %get-tuple-element.17) | copy-start | bytes 1179652
  351.8 70.1 %copy-start.4 = (f32[896,512]{1,0:T(8,128)S(1)}, f32[896,512]{1,0:T(8,128)}, u32[]{:S(2)}) copy-start(f32[896,512]{1,0:T(8,128)} %get-tuple-element.18) | copy-start | bytes 5505028
  449.5 1.1 slice-start
  453.4 12.9 %copy-start.2 = (f32[192,3072]{1,0:T(8,128)S(1)}, f32[192,3072]{1,0:T(8,128)}, u32[]{:S(2)}) copy-start(f32[192,3072]{1,0:T(8,128)} %copy-done.1) | copy-start | bytes 7077892
  453.4 12.9 %copy-start.12 = (f32[192,512]{1,0:T(8,128)S(1)}, f32[192,512]{1,0:T(8,128)}, u32[]{:S(2)}) copy-start(f32[192,512]{1,0:T(8,128)} %fusion.13) | copy-start | bytes 1179652
  466.2 5.8 %copy-start = (f32[512,3072]{1,0:T(8,128)}, f32[512,3072]{1,0:T(8,128)S(1)}, u32[]{:S(2)}) copy-start(f32[512,3072]{1,0:T(8,128)S(1)} %get-tuple-element.27) | copy-start | bytes 18874372
  481.6 6.4 %copy-start.5 = (f32[896,512]{1,0:T(8,128)S(1)}, f32[896,512]{1,0:T(8,128)}, u32[]{:S(2)}) copy-start(f32[896,512]{1,0:T(8,128)} %fusion.15) | copy-start | bytes 5505028
  481.6 6.4 %copy-start.11 = (f32[512,384]{1,0:T(8,128)S(1)}, f32[512,384]{1,0:T(8,128)}, u32[]{:S(2)}) copy-start(f32[512,384]{1,0:T(8,128)} %get-tuple-element.29) | copy-start | bytes 2359300
  487.1 1.6 copy-start.10
Sparse Core Ops, SparseCore 0:
  10.7 110.9 all-gather.4
  146.5 54.7 all-reduce.3
  261.3 70.9 all-gather.8
  342.7 106.8 all-gather.6
where the time goes:
time: 510 us; the launch traced here: 504 us
  waiting for transfers between devices  262 us (51%)
  matrix products  78.7 us (15%)
  Pallas kernels  68.2 us (13%)
  blocking collectives  53.9 us (11%)
  between operations  14.5 us (3%)
  other arithmetic  11.7 us (2%)
  local copies, waits for them, and re-layouts  10.3 us (2%)
  starting transfers between devices  5.27 us (1%)
    all_gather x1, waiting for transfers between devices, shards(): lax.all_gather(jnp.concatenate([basis_a, basis_b], axis=1), 'row', axis=0...  110 us
    dot_general x14, matrix products, dot(): lax.dot_general(x, y, (contract, ((), ())), precision=HIGHEST, preferred_...  78.7 us
    all_gather x1, waiting for transfers between devices, shards(): lax.all_gather(jnp.concatenate([proj_a, shares_b[:, :rank]]), 'row', axis=0)  70.7 us
    pallas_call x1, Pallas kernels, inverse_factors(): pl.pallas_call(functools.partial(inverse_kernel, rank), out_shape=[jax.Sh...  68.2 us
    psum x1, waiting for transfers between devices, shards(): proj_a, proj_b = lax.psum((partial_a, partial_b), 'col')  57.7 us
    all_to_all x1, blocking collectives, reduce_rows(): return jnp.sum(lax.all_to_all(shares, 'row', 0, 0), axis=0)  48 us
    all_gather x1, waiting for transfers between devices, shards(): lax.all_gather(jnp.concatenate([jnp.pad(block_a, ((0, 0), (0, width - wid...  23.2 us
  transfers between devices with their start and end apart: 5, of which 4 were waited for; matrix products, arithmetic and copies ran while one was open for 4% of the time, Pallas kernels for 14%

commit v1 on v0

v1 whole, which is shorter than its diff:
```python
import functools
import math

import jax
import jax.numpy as jnp
from jax import lax
from jax.experimental import pallas as pl
from jax.experimental.pallas import tpu as pltpu
from jax.sharding import PartitionSpec as P

MU = 0.95
EPS = 1e-06
BLOCK = 128
HIGHEST = lax.Precision.HIGHEST
MESH = pl.DeviceIdType.MESH
VMEM = pl.BlockSpec(memory_space=pltpu.VMEM)
DMA = pltpu.SemaphoreType.DMA
LAST = ((1,), (1,))
FIRST = ((0,), (0,))
PLAIN = ((1,), (0,))
SIDES = 2


def dot(x, y, contract=PLAIN, precision=HIGHEST):
    return lax.dot_general(
        x, y, (contract, ((), ())), precision=precision, preferred_element_type=jnp.float32
    )


def remote(src, dst, send, recv, device):
    return pltpu.make_async_remote_copy(
        src_ref=src,
        dst_ref=dst,
        send_sem=send,
        recv_sem=recv,
        device_id=device,
        device_id_type=MESH,
    )


def partner(position, bit):
    return position + bit - 2 * bit * lax.rem(position // bit, 2)


def col_bits(col_count):
    bits, bit = [], 1
    while bit < col_count:
        bits.append(bit)
        bit *= 2
    return bits


def greet_row(row, row_count, barrier):
    for k in range(1, row_count):
        peer = lax.rem(row + k, row_count)
        pl.semaphore_signal(barrier, inc=1, device_id={"row": peer}, device_id_type=MESH)


def greet_cols(col, bits, barrier):
    for bit in bits:
        peer = partner(col, bit)
        pl.semaphore_signal(barrier, inc=1, device_id={"col": peer}, device_id_type=MESH)


class Gather:
    def __init__(self, row_count, sources, outs, sems):
        self.depth = row_count // SIDES
        self.row = lax.axis_index("row")
        self.place = self.row // SIDES
        lane = lax.rem(self.row, SIDES)
        self.other = self.place * SIDES + (1 - lane)
        self.sources, self.outs = sources, outs
        self.up_s, self.up_r, self.dn_s, self.dn_r, self.side_s, self.side_r, self.own = sems
        self.has_up = self.place < self.depth - 1
        self.has_dn = self.place > 0

    @staticmethod
    def scratch(row_count, count):
        depth = row_count // SIDES
        line = DMA((count, depth))
        side = DMA((count, 2, depth))
        return [line, line, line, line, side, side, DMA((count,))]

    def up(self, i, slot, d, first=False):
        src = self.sources[i] if first else self.outs[i].at[slot]
        device = {"row": self.row + SIDES}
        return remote(src, self.outs[i].at[slot], self.up_s.at[i, d], self.up_r.at[i, d], device)

    def dn(self, i, slot, d, first=False):
        src = self.sources[i] if first else self.outs[i].at[slot]
        device = {"row": self.row - SIDES}
        return remote(src, self.outs[i].at[slot], self.dn_s.at[i, d], self.dn_r.at[i, d], device)

    def side(self, i, slot, way, d, first=False):
        src = self.sources[i] if first else self.outs[i].at[slot]
        sems = self.side_s.at[i, way, d], self.side_r.at[i, way, d]
        return remote(src, self.outs[i].at[slot], *sems, {"row": self.other})

    def local(self, i):
        return pltpu.make_async_copy(self.sources[i], self.outs[i].at[self.row], self.own.at[i])

    def each(self):
        return range(len(self.sources))

    def start(self):
        for i in self.each():

            @pl.when(self.has_up)
            def _():
                self.up(i, self.row, 0, True).start()

            @pl.when(self.has_dn)
            def _():
                self.dn(i, self.row, 0, True).start()

            self.side(i, self.row, 0, 0, True).start()
        for i in self.each():
            self.local(i).start()

    def below(self, d):
        return self.row - d * SIDES

    def above(self, d):
        return self.row + d * SIDES

    def has_below(self, d):
        return self.place - d >= 0

    def has_above(self, d):
        return self.place + d < self.depth

    def forward(self, d):
        low, high = self.below(d), self.above(d)

        @pl.when(self.has_below(d))
        def _():
            for i in self.each():
                self.up(i, low, d - 1).wait_recv()

                @pl.when(self.has_up)
                def _():
                    self.up(i, low, d).start()

                self.side(i, low, 0, d).start()

        @pl.when(self.has_above(d))
        def _():
            for i in self.each():
                self.dn(i, high, d - 1).wait_recv()

                @pl.when(self.has_dn)
                def _():
                    self.dn(i, high, d).start()

                self.side(i, high, 1, d).start()

    def across(self, way, d):
        step = d * SIDES
        return self.other + (step if way else -step)

    def wait_side(self, way, d):
        for i in self.each():
            self.side(i, self.across(way, d), way, d).wait_recv()

    def drain(self):
        for i in self.each():

            @pl.when(self.has_up)
            def _():
                self.up(i, self.row, 0, True).wait_send()

            @pl.when(self.has_dn)
            def _():
                self.dn(i, self.row, 0, True).wait_send()

            self.side(i, self.row, 0, 0, True).wait_send()

        def later(d, carry):
            for i in self.each():

                @pl.when(self.has_below(d))
                def _():
                    @pl.when(self.has_up)
                    def _():
                        self.up(i, self.below(d), d).wait_send()

                    self.side(i, self.below(d), 0, d).wait_send()

                @pl.when(self.has_above(d))
                def _():
                    @pl.when(self.has_dn)
                    def _():
                        self.dn(i, self.above(d), d).wait_send()

                    self.side(i, self.above(d), 1, d).wait_send()

            return carry

        lax.fori_loop(1, self.depth, later, 0)


class ColSum:
    def __init__(self, bits, sums, landed, send, recv):
        self.bits, self.sums, self.landed, self.send, self.recv = bits, sums, landed, send, recv
        self.col = lax.axis_index("col")

    def copy(self, stage):
        device = {"col": partner(self.col, self.bits[stage])}
        sems = self.send.at[stage], self.recv.at[stage]
        return remote(self.sums[stage], self.landed[stage], *sems, device)

    def finish(self, stage):
        self.copy(stage).wait_recv()
        self.sums[stage + 1][...] = self.sums[stage][...] + self.landed[stage][...]

    def drain(self):
        for stage in range(len(self.bits)):
            self.copy(stage).wait_send()


def project_kernel(row_count, bits, *refs):
    stages = len(bits)
    basis_a, basis_b, buffer_a, buffer_b, cut_a, out_a, out_b, tall = refs[:8]
    all_a, all_b = refs[8:10]
    sums_a = list(refs[10 : 10 + stages]) + [out_a]
    sums_b = list(refs[10 + stages : 10 + 2 * stages]) + [out_b]
    landed_a = refs[10 + 2 * stages : 10 + 3 * stages]
    landed_b = refs[10 + 3 * stages : 10 + 4 * stages]
    gather_sems = refs[10 + 4 * stages : 17 + 4 * stages]
    small_s, small_r, small_own, cut_s, cut_r, cut_own = refs[17 + 4 * stages : 23 + 4 * stages]
    cs_a, cr_a, cs_b, cr_b = refs[23 + 4 * stages :]
    row, col = lax.axis_index("row"), lax.axis_index("col")
    share = basis_a.shape[0]
    depth = row_count // SIDES

    barrier = pltpu.get_barrier_semaphore()
    greet_row(row, row_count, barrier)
    greet_cols(col, bits, barrier)
    pl.semaphore_wait(barrier, row_count - 1 + stages)

    def small(k):
        peer = lax.rem(row + k, row_count)
        return remote(basis_b, all_b.at[row], small_s.at[k], small_r.at[k], {"row": peer})

    def cut(k):
        peer = lax.rem(row + k, row_count)
        return remote(cut_a.at[peer], tall.at[row], cut_s.at[k], cut_r.at[k], {"row": peer})

    small_local = pltpu.make_async_copy(basis_b, all_b.at[row], small_own)
    cut_local = pltpu.make_async_copy(cut_a.at[row], tall.at[row], cut_own)
    for k in range(1, row_count):
        small(k).start()
    gather = Gather(row_count, [basis_a], [all_a], gather_sems)
    gather.start()
    small_local.start()
    cut_local.start()

    def project(slot):
        rows = pl.ds(pl.multiple_of(slot * share, share), share)
        sums_a[0][rows, :] = dot(all_a[slot], buffer_a[...], LAST)

    gather.local(0).wait()
    project(row)
    small_local.wait()
    for k in range(1, row_count):
        small(k).wait_recv()
    for k in range(row_count):
        sums_b[0][k * share : (k + 1) * share, :] = dot(all_b[k], buffer_b[...], LAST)
    total_a = ColSum(bits, sums_a, landed_a, cs_a, cr_a)
    total_b = ColSum(bits, sums_b, landed_b, cs_b, cr_b)
    total_b.copy(0).start()

    def advance(d, carry):
        gather.forward(d)

        @pl.when(d == min(2, depth - 1))
        def _():
            for k in range(1, row_count):
                cut(k).start()

        @pl.when(gather.has_below(d - 1))
        def _():
            gather.wait_side(0, d - 1)

        @pl.when((d > 1) & gather.has_above(d - 1))
        def _():
            gather.wait_side(1, d - 1)

        def use(k, inner):
            line, way = k // 2, lax.rem(k, 2)
            step = (d - line) * (2 * way - 1)
            there = gather.place + step
            here = (there >= 0) & (there < depth) & ((way == 0) | (d - line > 0))

            @pl.when(here)
            def _():
                base = gather.row + line * (gather.other - gather.row)
                project(base + step * SIDES)

            return inner

        lax.fori_loop(0, 4, use, 0)
        return carry

    lax.fori_loop(1, depth, advance, 0)
    for stage in range(stages):
        total_b.finish(stage)
        if stage + 1 < stages:
            total_b.copy(stage + 1).start()

    def finish(way, carry):
        step = (depth - 1) * (2 * way - 1)
        there = gather.place + step

        @pl.when((there >= 0) & (there < depth))
        def _():
            project(gather.other + step * SIDES)

        return carry

    @pl.when(gather.has_below(depth - 1))
    def _():
        gather.wait_side(0, depth - 1)

    @pl.when(gather.has_above(depth - 1))
    def _():
        gather.wait_side(1, depth - 1)

    lax.fori_loop(0, 2, finish, 0)
    for stage in range(stages):
        total_a.copy(stage).start()
        total_a.finish(stage)
    cut_local.wait()
    for k in range(1, row_count):
        cut(k).wait()
        small(k).wait_send()
    gather.drain()
    total_a.drain()
    total_b.drain()


def project(basis_a, basis_b, buffer_a, buffer_b, cut_a):
    row_count, col_count = lax.axis_size("row"), lax.axis_size("col")
    bits = col_bits(col_count)
    stages = len(bits)
    share, rows_a, rows_b = basis_a.shape[0], buffer_a.shape[0], buffer_b.shape[0]
    rank = share * row_count
    float_a, float_b = (
        jax.ShapeDtypeStruct((rank, rows_a), jnp.float32),
        jax.ShapeDtypeStruct((rank, rows_b), jnp.float32),
    )
    space_a, space_b = pltpu.VMEM(float_a.shape, jnp.float32), pltpu.VMEM(float_b.shape, jnp.float32)
    return pl.pallas_call(
        functools.partial(project_kernel, row_count, bits),
        out_shape=[float_a, float_b, jax.ShapeDtypeStruct(cut_a.shape, jnp.float32)],
        in_specs=[VMEM] * 5,
        out_specs=[VMEM] * 3,
        scratch_shapes=[
            pltpu.VMEM((row_count,) + basis_a.shape, jnp.float32),
            pltpu.VMEM((row_count,) + basis_b.shape, jnp.float32),
        ]
        + [space_a] * stages
        + [space_b] * stages
        + [space_a] * stages
        + [space_b] * stages
        + Gather.scratch(row_count, 1)
        + [DMA((row_count,)), DMA((row_count,)), DMA(())] * 2
        + [DMA((stages,))] * 4,
        name="project",
        compiler_params=pltpu.CompilerParams(
            collective_id=1, has_side_effects=True, vmem_limit_bytes=60 * 2**20
        ),
    )(basis_a, basis_b, buffer_a, buffer_b, cut_a)


def factor(rank, grams, outs, works, diags, between):
    eye_rows = lax.broadcasted_iota(jnp.int32, (rank, rank), 0)
    eye_cols = lax.broadcasted_iota(jnp.int32, (rank, rank), 1)
    for gram, work in zip(grams, works):
        work[:, :rank] = gram[...]
        work[:, rank:] = (eye_rows == eye_cols).astype(jnp.float32)
    rows = lax.broadcasted_iota(jnp.int32, (BLOCK, 1), 0)
    lanes = lax.broadcasted_iota(jnp.int32, (1, BLOCK), 1)
    for k in range(rank // BLOCK):
        low, high = k * BLOCK, (k + 1) * BLOCK
        for work, diag in zip(works, diags):
            diag[:, :BLOCK] = work[low:high, low:high]
            diag[:, BLOCK:] = (rows == lanes).astype(jnp.float32)

        def step(j, carry):
            for diag in diags:
                here = lanes == j
                row = diag[pl.ds(j, 1), :]
                col = jnp.sum(jnp.where(here, diag[:, :BLOCK], 0.0), axis=1, keepdims=True)
                pivot = jnp.sum(jnp.where(here, row[:, :BLOCK], 0.0), axis=1, keepdims=True)
                factor = jnp.where(rows > j, col * (1.0 / pivot), 0.0)
                diag[...] = diag[...] - factor * row
            return carry

        lax.fori_loop(0, BLOCK, step, 0)
        width = slice(low, rank + high)
        for work, diag in zip(works, diags):
            pivots = jnp.sum(
                jnp.where(rows == lanes, diag[:, :BLOCK], 0.0), axis=1, keepdims=True
            )
            inverse = diag[:, BLOCK:] * (1.0 / jnp.sqrt(pivots))
            panel = dot(inverse, work[low:high, width])
            work[low:high, width] = panel
            if high < rank:
                factors = panel[:, BLOCK : rank - low]
                work[high:, width] = work[high:, width] - dot(factors, panel, FIRST)
        between(k)
    for work, out in zip(works, outs):
        out[...] = work[:, rank:]


def products_kernel(row_count, rank, *refs):
    gram_a, gram_b, block_a, block_b, inv_a, inv_b, all_a, all_b = refs[:8]
    works, diags, sems = refs[8:10], refs[10:12], refs[12:19]
    row = lax.axis_index("row")
    barrier = pltpu.get_barrier_semaphore()
    greet_row(row, row_count, barrier)
    pl.semaphore_wait(barrier, row_count - 1)
    gather = Gather(row_count, [block_a, block_b], [all_a, all_b], sems)
    gather.start()
    early = min(rank // BLOCK, gather.depth)

    def between(k):
        if k + 1 < early:
            gather.forward(k + 1)

    factor(rank, [gram_a, gram_b], [inv_a, inv_b], works, diags, between)

    def later(d, carry):
        gather.forward(d)
        return carry

    lax.fori_loop(early, gather.depth, later, 0)
    gather.wait_side(0, 0)

    def landed(d, carry):
        @pl.when(gather.has_below(d))
        def _():
            gather.wait_side(0, d)

        @pl.when(gather.has_above(d))
        def _():
            gather.wait_side(1, d)

        return carry

    lax.fori_loop(1, gather.depth, landed, 0)
    for i in gather.each():
        gather.local(i).wait()
    gather.drain()


def products(gram_a, gram_b, block_a, block_b):
    row_count = lax.axis_size("row")
    rank = gram_a.shape[0]
    square = jax.ShapeDtypeStruct((rank, rank), jnp.float32)
    return pl.pallas_call(
        functools.partial(products_kernel, row_count, rank),
        out_shape=[square, square]
        + [jax.ShapeDtypeStruct((row_count,) + x.shape, jnp.float32) for x in (block_a, block_b)],
        in_specs=[VMEM] * 4,
        out_specs=[VMEM] * 4,
        scratch_shapes=[pltpu.VMEM((rank, 2 * rank), jnp.float32)] * 2
        + [pltpu.VMEM((BLOCK, 2 * BLOCK), jnp.float32)] * 2
        + Gather.scratch(row_count, 2),
        name="products",
        compiler_params=pltpu.CompilerParams(
            collective_id=2, has_side_effects=True, vmem_limit_bytes=60 * 2**20
        ),
    )(gram_a, gram_b, block_a, block_b)


def reduce_rows(partial_sum):
    share_count = lax.axis_size("row")
    shares = partial_sum.reshape(share_count, -1, partial_sum.shape[1])
    return jnp.sum(lax.all_to_all(shares, "row", 0, 0), axis=0)


def shards(mom_a, grad_a, basis_a, mom_b, grad_b, basis_b):
    row_count = lax.axis_size("row")
    buffer_a, buffer_b = MU * mom_a + grad_a, MU * mom_b + grad_b
    rows_a = buffer_a.shape[0]
    cut_a = buffer_a.reshape(rows_a, row_count, -1).swapaxes(0, 1)
    proj_a, proj_b, tall_a = project(basis_a, basis_b, buffer_a, buffer_b, cut_a)
    rank = proj_a.shape[0]
    share = rank // row_count

    shares_b = reduce_rows(
        jnp.concatenate([dot(proj_b, proj_b, LAST), dot(proj_b, buffer_b)], axis=1)
    )
    share_b = shares_b[:, rank:]
    all_a = lax.all_gather(proj_a, "row", axis=0)
    gram_b = lax.all_gather(shares_b[:, :rank], "row", axis=0, tiled=True)
    all_a = all_a.swapaxes(0, 1).reshape(rank, -1)
    gram_a = dot(all_a, all_a, LAST)
    block_a = dot(all_a, tall_a.reshape(-1, tall_a.shape[2]))
    inverse_a, inverse_b, product_a, product_b = products(gram_a, gram_b, block_a, share_b)
    product_a = product_a.swapaxes(0, 1).reshape(rank, -1)
    product_b = product_b.reshape(rank, -1)

    ortho_a, ortho_b = dot(proj_a, inverse_a, ((0,), (1,))), dot(proj_b, inverse_b, ((0,), (1,)))
    trans_a, trans_b = dot(inverse_a, product_a), dot(inverse_b, product_b)
    squares_a, squares_b = lax.psum(
        (
            jnp.sum(trans_a * trans_a, axis=1, keepdims=True),
            jnp.sum(trans_b * trans_b, axis=1, keepdims=True),
        ),
        "col",
    )
    start = lax.axis_index("row") * share
    first_out = finish(buffer_a, ortho_a, trans_a, squares_a, start, share)
    second_out = finish(buffer_b, ortho_b, trans_b, squares_b, start, share)
    return (*first_out, *second_out)


def finish(buffer, ortho, trans, squares, start, share):
    rank = ortho.shape[1]
    total_rows = buffer.shape[0] * lax.axis_size("row")
    total_cols = buffer.shape[1] * lax.axis_size("col")
    full_basis = trans / jnp.sqrt(squares + EPS)
    own_basis = lax.dynamic_slice_in_dim(full_basis, start, share, 0)
    new_mom = buffer - (1.0 - MU) * dot(ortho, trans)
    update = dot(ortho, full_basis) * math.sqrt(total_rows * total_cols / rank)
    return new_mom, update.astype(jnp.bfloat16), own_basis


def solution(mesh):
    spec = P("row", "col")
    return jax.shard_map(
        shards, mesh=mesh, in_specs=(spec,) * 6, out_specs=(spec,) * 6, check_vma=False
    )
```

time: 510 us -> 493 us (0.967)
  waiting for transfers between devices: 262 us -> 19.3 us
  Pallas kernels: 68.2 us -> 240 us
  blocking collectives: 53.9 us -> 106 us
  local copies, waits for them, and re-layouts: 10.3 us -> 21 us
  matrix products: 78.7 us -> 73.4 us
  starting transfers between devices: 5.27 us -> 0.08 us
    all_gather x3 -> x2, waiting for transfers between devices: 204 us -> 19.3 us  [the longest x1 17.2 us: shards(): gram_b = lax.all_gather(shares_b[:, :rank], 'row', axis=0, tiled=True)]
    pallas_call x1 -> x2, Pallas kernels: 68.2 us -> 240 us  [the longest x1 156 us: project(): pl.pallas_call(functools.partial(project_kernel, row_count, bits), out_sh...]
    psum x1 -> x0, waiting for transfers between devices: 57.7 us -> none  [shards(): proj_a, proj_b = lax.psum((partial_a, partial_b), 'col')]
    all_to_all x1, blocking collectives: 48 us -> 100 us  [reduce_rows(): return jnp.sum(lax.all_to_all(shares, 'row', 0, 0), axis=0)]
    transpose x0 -> x1, local copies, waits for them, and re-layouts: none -> 6.56 us  [shards(): product_a = product_a.swapaxes(0, 1).reshape(rank, -1)]
    dot_general x14 -> x12, matrix products: 78.7 us -> 73.4 us  [dot(): lax.dot_general(x, y, (contract, ((), ())), precision=precision, preferre...]
    all_gather x0 -> x1, local copies, waits for them, and re-layouts: none -> 5.23 us  [shards(): all_a = lax.all_gather(proj_a, 'row', axis=0)]
  transfers between devices with their start and end apart: 5 -> 2, of which waited for: 4 -> 2; matrix products, arithmetic and copies ran while one was open for 4% -> 8% of each run, Pallas kernels for 14% -> 0%
where the time goes in v1:
time: 493 us; the launch traced here: 484 us
  Pallas kernels  240 us (49%)
  blocking collectives  106 us (22%)
  matrix products  73.4 us (15%)
  local copies, waits for them, and re-layouts  21 us (4%)
  waiting for transfers between devices  19.3 us (4%)
  between operations  14.4 us (3%)
  other arithmetic  10.8 us (2%)
    pallas_call x1, Pallas kernels, project(): pl.pallas_call(functools.partial(project_kernel, row_count, bits), out_sh...  156 us
    all_to_all x1, blocking collectives, reduce_rows(): return jnp.sum(lax.all_to_all(shares, 'row', 0, 0), axis=0)  100 us
    pallas_call x1, Pallas kernels, products(): pl.pallas_call(functools.partial(products_kernel, row_count, rank), out_s...  83.6 us
    dot_general x12, matrix products, dot(): lax.dot_general(x, y, (contract, ((), ())), precision=precision, preferre...  73.4 us
    all_gather x1, waiting for transfers between devices, shards(): gram_b = lax.all_gather(shares_b[:, :rank], 'row', axis=0, tiled=True)  17.2 us
  transfers between devices with their start and end apart: 2, of which 2 were waited for; matrix products, arithmetic and copies ran while one was open for 8% of the time, Pallas kernels for 0%

profile of v1, /device:TPU:0, one launch (start us, length us, event | category | flops | bytes accessed | tf_op | source)
XLA Modules:
  0.0 484.5 jit_solution(6687188163381968523)
XLA Ops:
  7.2 2.7 multiply_add_fusion.refs_2_
  14.7 156.1 %project.1 = (f32[512,192]{1,0:T(8,128)}, f32[512,896]{1,0:T(8,128)}, f32[8,192,384]{2,1,0:T(8,128)}) custom-call(f32[64,3072]{1,0:T(8,128)} %refs_0_.1, f32[64,384]{1,0:T(8,128)} %refs_1_.1, f32[192,3072]{1,0:T(8,128)} %copy-done.1, f32[896,384]{1,0:T(8,128)} %multiply_add_fusion.1.refs_3_, f32[8,192,384]{2,1,0:T(8,128)} %bitcast.52), custom_call_target="tpu_custom_call" | custom-call | tf_op jit(solution)/shard_map/project/pallas_call | solution.py:353
  170.9 4.3 fusion.15
  175.2 3.5 fusion.14
  180.1 2.8 copy.15
  182.8 100.0 %all_to_all.5 = f32[8,64,896]{2,1,0:T(8,128)} all-to-all(f32[8,64,896]{2,1,0:T(8,128)} %bitcast.53), channel_id=1, replica_groups=mesh['row'=8,'col'=4] {'row'}, dimensions={0} | all-to-all | bytes 3670016 | tf_op jit(solution)/shard_map/all_to_all | solution.py:481
  282.8 1.6 reduce_sum.27
  285.7 2.1 all-gather.6.cloned.1.call-done
  287.9 5.2 %copy.14 = f32[8,512,192]{1,2,0:T(8,128)} copy(f32[8,512,192]{2,1,0:T(8,128)} %bitcast.55) | data formatting | bytes 6291456 | tf_op jit(solution)/shard_map/all_gather | solution.py:497
  293.1 13.4 %fusion.7.refs_0_ = f32[512,512]{1,0:T(8,128)} fusion(f32[8,512,192]{1,2,0:T(8,128)} %copy.14), kind=kOutput, calls=%fused_computation.17 | convolution fusion | flops 4831838208 | bytes 4194304 | tf_op jit(solution)/shard_map/dot_general | solution.py:25
  306.5 6.1 %fusion.11.refs_2_ = f32[512,384]{1,0:T(8,128)} fusion(f32[8,192,384]{2,1,0:T(8,128)S(1)} %copy-done.11, f32[8,512,192]{1,2,0:T(8,128)S(1)} %copy-done.6), kind=kOutput, calls=%fused_computation.19 | convolution fusion | flops 3623878656 | bytes 6291456 | tf_op jit(solution)/shard_map/dot_general | solution.py:25
  312.6 17.2 %all-gather.4.cloned.1.call-done.refs_1_ = f32[512,512]{1,0:T(8,128)} async-done(((f32[64,512]{1,0:T(8,128)}), f32[512,512]{1,0:T(8,128)}) %all-gather.4.cloned.1.call-update) | async-done | bytes 1048592 | tf_op jit(solution)/shard_map/all_gather | solution.py:498
  329.8 83.6 %products.1 = (f32[512,512]{1,0:T(8,128)}, f32[512,512]{1,0:T(8,128)}, f32[8,512,384]{2,1,0:T(8,128)}, f32[8,64,384]{2,1,0:T(8,128)}) custom-call(f32[512,512]{1,0:T(8,128)} %fusion.7.refs_0_, f32[512,512]{1,0:T(8,128)} %all-gather.4.cloned.1.call-done.refs_1_, f32[512,384]{1,0:T(8,128)} %fusion.11.refs_2_, f32[64,384]{1,0:T(8,128)} %slice.9.refs_3_), custom_call_target="tpu_custom_call" | custom-call | tf_op jit(solution)/shard_map/products/pallas_call | solution.py:462
  413.5 3.8 fusion.16
  417.3 6.6 %copy.16 = f32[512,8,384]{0,2,1:T(8,128)} copy(f32[512,8,384]{2,0,1:T(8,128)} %bitcast.54) | data formatting | bytes 12582912 | tf_op jit(solution)/shard_map/transpose | solution.py:503
  423.9 13.2 %multiply_reduce_fusion = (f32[512]{0:T(512)S(1)}, f32[512,3072]{1,0:T(8,128)S(1)}) fusion(f32[512,512]{1,0:T(8,128)} %get-tuple-element.16, f32[512,3072]{0,1:T(8,128)} %bitcast.51), kind=kOutput, calls=%fused_computation | convolution fusion | flops 9666822144 | bytes 13633536 | tf_op jit(solution)/shard_map/dot_general | solution.py:25
  437.2 7.1 %fusion.17 = f32[896,512]{1,0:T(8,128)} fusion(f32[512,896]{1,0:T(8,128)S(1)} %copy-done.3, f32[512,512]{1,0:T(8,128)S(1)} %copy-done.8), kind=kOutput, calls=%fused_computation.29 | convolution fusion | flops 2818572288 | bytes 4718592 | tf_op jit(solution)/shard_map/dot_general | solution.py:25
  444.3 2.7 multiply_reduce_fusion.1
  447.0 5.8 %fusion = f32[192,3072]{1,0:T(8,128)} fusion(f32[192,3072]{1,0:T(8,128)S(1)} %copy-done.2, f32[192,512]{1,0:T(8,128)S(1)} %copy-done.9, f32[512,3072]{1,0:T(8,128)S(1)} %get-tuple-element.23), kind=kOutput, calls=%fused_computation.3 | convolution fusion | flops 3625058304 | bytes 11403264 | tf_op jit(solution)/shard_map/dot_general | solution.py:25
  452.8 5.8 %all-reduce = (f32[512,1]{0,1:T(1,128)S(1)}, f32[512,1]{0,1:T(1,128)S(1)}) all-reduce(f32[512,1]{0,1:T(1,128)S(1)} %bitcast.57, f32[512,1]{0,1:T(1,128)S(1)} %bitcast.59), channel_id=1, replica_groups=mesh['row'=8,'col'=4] {'col'}, use_global_device_ids=true, to_apply=%region_2.0 | all-reduce | flops 1024 | bytes 8192 | tf_op jit(solution)/shard_map/psum | solution.py:508
  458.6 3.7 broadcast_divide_fusion
  462.3 5.4 %fusion.1 = bf16[192,3072]{1,0:T(8,128)(2,1)} fusion(f32[192,512]{1,0:T(8,128)S(1)} %copy-done.10, f32[512,3072]{1,0:T(8,128)S(1)} %broadcast_divide_fusion), kind=kOutput, calls=%fused_computation.4 | convolution fusion | flops 3625058304 | bytes 7864320 | tf_op jit(solution)/shard_map/dot_general | solution.py:25
  468.7 4.1 fusion.6
  472.9 3.9 fusion.10
  (45 shorter events, 9.3 us)
Async XLA Ops:
  7.2 280.7 %all-gather.6.cloned.1.call-start = ((), (), s32[]{:S(2)}) async-start(), calls=%async_computation.2 | async-start | bytes 4718592 | tf_op jit(solution)/shard_map/all_gather | solution.py:497
  10.0 2.4 copy-start.1
  10.0 2.4 copy-start.13
  10.0 3.4 copy-start.14
  14.7 156.2 %copy-start.4 = (f32[896,384]{1,0:T(8,128)S(1)}, f32[896,384]{1,0:T(8,128)}, u32[]{:S(2)}) copy-start(f32[896,384]{1,0:T(8,128)} %multiply_add_fusion.1.refs_3_) | copy-start | bytes 4128772
  170.8 4.4 copy-start.3
  170.8 159.0 %all-gather.4.cloned.1.call-start = ((), (), s32[]{:S(2)}) async-start(), calls=%async_computation.1 | async-start | bytes 1179648 | tf_op jit(solution)/shard_map/all_gather | solution.py:498
  293.1 13.4 %copy-start.6 = (f32[8,512,192]{1,2,0:T(8,128)S(1)}, f32[8,512,192]{1,2,0:T(8,128)}, u32[]{:S(2)}) copy-start(f32[8,512,192]{1,2,0:T(8,128)} %copy.14) | copy-start | bytes 9437188
  293.1 13.4 %copy-start.11 = (f32[8,192,384]{2,1,0:T(8,128)S(1)}, f32[8,192,384]{2,1,0:T(8,128)}, u32[]{:S(2)}) copy-start(f32[8,192,384]{2,1,0:T(8,128)} %get-tuple-element.15) | copy-start | bytes 7077892
  329.8 83.7 %copy-start.12 = (f32[512,192]{1,0:T(8,128)S(1)}, f32[512,192]{1,0:T(8,128)}, u32[]{:S(2)}) copy-start(f32[512,192]{1,0:T(8,128)} %get-tuple-element.13) | copy-start | bytes 1179652
  423.9 13.3 %copy-start.8 = (f32[512,512]{1,0:T(8,128)S(1)}, f32[512,512]{1,0:T(8,128)}, u32[]{:S(2)}) copy-start(f32[512,512]{1,0:T(8,128)} %get-tuple-element.18) | copy-start | bytes 3145732
  437.1 9.9 %copy-start = (f32[512,3072]{1,0:T(8,128)}, f32[512,3072]{1,0:T(8,128)S(1)}, u32[]{:S(2)}) copy-start(f32[512,3072]{1,0:T(8,128)S(1)} %get-tuple-element.23) | copy-start | bytes 18874372
  437.1 7.2 %copy-start.15 = (f32[8,64,384]{2,1,0:T(8,128)S(1)}, f32[8,64,384]{2,1,0:T(8,128)}, u32[]{:S(2)}) copy-start(f32[8,64,384]{2,1,0:T(8,128)} %get-tuple-element.19) | copy-start | bytes 2359300
  437.1 9.8 %copy-start.9 = (f32[192,512]{1,0:T(8,128)S(1)}, f32[192,512]{1,0:T(8,128)}, u32[]{:S(2)}) copy-start(f32[192,512]{1,0:T(8,128)} %fusion.16) | copy-start | bytes 1179652
  444.3 2.7 copy-start.2
  458.6 3.7 copy-start.10
  462.3 6.4 %copy-start.5 = (f32[896,512]{1,0:T(8,128)S(1)}, f32[896,512]{1,0:T(8,128)}, u32[]{:S(2)}) copy-start(f32[896,512]{1,0:T(8,128)} %fusion.17) | copy-start | bytes 5505028
  462.3 6.4 %copy-start.7 = (f32[512,384]{1,0:T(8,128)S(1)}, f32[512,384]{1,0:T(8,128)}, u32[]{:S(2)}) copy-start(f32[512,384]{1,0:T(8,128)} %get-tuple-element.25) | copy-start | bytes 2359300
Sparse Core Ops, SparseCore 0:
  170.9 116.9 all-gather.5
  290.6 39.2 all-gather.3

commit v2 on v0

v2 whole, which is shorter than its diff:
```python
import functools
import math

import jax
import jax.numpy as jnp
from jax import lax
from jax.experimental import pallas as pl
from jax.experimental.pallas import tpu as pltpu
from jax.sharding import PartitionSpec as P

MU = 0.95
EPS = 1e-06
BLOCK = 128
HIGHEST = lax.Precision.HIGHEST
MESH = pl.DeviceIdType.MESH
VMEM = pl.BlockSpec(memory_space=pltpu.VMEM)
DMA = pltpu.SemaphoreType.DMA
LAST = ((1,), (1,))
FIRST = ((0,), (0,))
PLAIN = ((1,), (0,))
SIDES = 2
PIECES = 2
CHUNK = 256


def dot(x, y, contract=PLAIN, precision=HIGHEST):
    return lax.dot_general(
        x, y, (contract, ((), ())), precision=precision, preferred_element_type=jnp.float32
    )


def halves(x):
    high = x.astype(jnp.bfloat16)
    return high, (x - high.astype(jnp.float32)).astype(jnp.bfloat16)


def narrow_dot(x, y, contract=PLAIN):
    return lax.dot_general(x, y, (contract, ((), ())), preferred_element_type=jnp.float32)


def split_dot(x, y, contract=PLAIN):
    (x_high, x_low), (y_high, y_low) = halves(x), halves(y)
    total = narrow_dot(x_high, y_low, contract) + narrow_dot(x_low, y_high, contract)
    return total + narrow_dot(x_high, y_high, contract)


def remote(src, dst, send, recv, device):
    return pltpu.make_async_remote_copy(
        src_ref=src,
        dst_ref=dst,
        send_sem=send,
        recv_sem=recv,
        device_id=device,
        device_id_type=MESH,
    )


def partner(position, bit):
    return position + bit - 2 * bit * lax.rem(position // bit, 2)


def col_bits(col_count):
    bits, bit = [], 1
    while bit < col_count:
        bits.append(bit)
        bit *= 2
    return bits


def greet_row(row, row_count, barrier):
    for k in range(1, row_count):
        peer = lax.rem(row + k, row_count)
        pl.semaphore_signal(barrier, inc=1, device_id={"row": peer}, device_id_type=MESH)


def greet_cols(col, bits, barrier):
    for bit in bits:
        peer = partner(col, bit)
        pl.semaphore_signal(barrier, inc=1, device_id={"col": peer}, device_id_type=MESH)


class Line:
    def __init__(self, row_count, sources, outs, sems):
        self.depth = row_count // SIDES
        self.row = lax.axis_index("row")
        self.place = self.row // SIDES
        self.sources, self.outs = sources, outs
        self.up_s, self.up_r, self.dn_s, self.dn_r = sems
        self.has_up = self.place < self.depth - 1
        self.has_dn = self.place > 0

    @staticmethod
    def scratch(row_count, count):
        return [DMA((count, row_count // SIDES))] * 4

    def up(self, i, slot, d, first=False):
        src = self.sources[i] if first else self.outs[i].at[slot]
        device = {"row": self.row + SIDES}
        return remote(src, self.outs[i].at[slot], self.up_s.at[i, d], self.up_r.at[i, d], device)

    def dn(self, i, slot, d, first=False):
        src = self.sources[i] if first else self.outs[i].at[slot]
        device = {"row": self.row - SIDES}
        return remote(src, self.outs[i].at[slot], self.dn_s.at[i, d], self.dn_r.at[i, d], device)

    def has(self, way, d):
        there = self.place + d * (2 * way - 1)
        return (d >= 0) & (there >= 0) & (there < self.depth) & ((way == 0) | (d > 0))

    def start(self, i):
        @pl.when(self.has_up)
        def _():
            self.up(i, self.place, 0, True).start()

        @pl.when(self.has_dn)
        def _():
            self.dn(i, self.place, 0, True).start()

    def forward(self, d):
        for i in range(len(self.outs)):

            @pl.when(self.has(0, d))
            def _():
                self.up(i, self.place - d, d - 1).wait_recv()

                @pl.when(self.has_up)
                def _():
                    self.up(i, self.place - d, d).start()

            @pl.when(self.has(1, d))
            def _():
                self.dn(i, self.place + d, d - 1).wait_recv()

                @pl.when(self.has_dn)
                def _():
                    self.dn(i, self.place + d, d).start()

    def drain(self):
        def sent(d, carry):
            for i in range(len(self.outs)):

                @pl.when((self.place - d >= 0) & self.has_up)
                def _():
                    self.up(i, self.place - d, d).wait_send()

                @pl.when((self.place + d < self.depth) & self.has_dn)
                def _():
                    self.dn(i, self.place + d, d).wait_send()

            return carry

        lax.fori_loop(0, self.depth, sent, 0)


def project_kernel(row_count, bits, *refs):
    basis_a, basis_b, buffer_a, buffer_b, proj_a, proj_b, pair = refs[:7]
    mine, theirs, all_b, high, low, part_b, land_b = refs[7:14]
    refs = refs[14:]
    stages = len(bits) + 1
    sums, refs = list(refs[:stages]) + [proj_a], refs[stages:]
    landed, refs = refs[:stages], refs[stages:]
    sums_b, refs = refs[: len(bits)], refs[len(bits) :]
    landed_b, refs = refs[: len(bits) - 1], refs[len(bits) - 1 :]
    line_sems, refs = refs[:4], refs[4:]
    small_s, small_r, small_own, swap_s, swap_r, swap_own, sum_s, sum_r, b_s, b_r = refs
    row, col = lax.axis_index("row"), lax.axis_index("col")
    place, lane = row // SIDES, lax.rem(row, SIDES)
    other = place * SIDES + (1 - lane)
    share, width = basis_a.shape[0], mine.shape[2]
    depth = row_count // SIDES
    rank = share * row_count
    half = rank // 2
    twin, part = partner(col, 1), lax.rem(col, 2)
    devices = [{"col": partner(col, bit)} for bit in bits] + [{"row": other}]

    barrier = pltpu.get_barrier_semaphore()
    greet_row(row, row_count, barrier)
    greet_cols(col, bits, barrier)
    pl.semaphore_wait(barrier, row_count - 1 + len(bits))

    def columns(position):
        return pl.ds(pl.multiple_of(position * width, width), width)

    def small(k):
        peer = lax.rem(row + k, row_count)
        return remote(basis_b, all_b.at[row], small_s.at[k], small_r.at[k], {"row": peer})

    swap_basis = remote(
        basis_a.at[:, columns(1 - lane)], theirs.at[place], swap_s.at[0], swap_r.at[0], {"row": other}
    )
    swap_rows = remote(
        buffer_a.at[:, columns(1 - lane)], pair.at[lane], swap_s.at[1], swap_r.at[1], {"row": other}
    )
    own_basis = pltpu.make_async_copy(basis_a.at[:, columns(lane)], mine.at[place], swap_own.at[0])
    own_rows = pltpu.make_async_copy(buffer_a.at[:, columns(lane)], pair.at[lane], swap_own.at[1])
    small_local = pltpu.make_async_copy(basis_b, all_b.at[row], small_own)
    sources = [basis_a.at[:, columns(lane)], theirs.at[place]]
    line = Line(row_count, sources, [mine, theirs], line_sems)
    swap_basis.start()
    line.start(0)
    for k in range(1, row_count):
        small(k).start()
    swap_rows.start()
    own_basis.start()
    own_rows.start()
    small_local.start()

    def unit(place_):
        return pl.ds(pl.multiple_of(place_ * SIDES * share, SIDES * share), SIDES * share)

    def summing(stage, place_):
        sems = sum_s.at[stage, place_], sum_r.at[stage, place_]
        here, there = sums[stage].at[unit(place_), :], landed[stage].at[unit(place_), :]
        return remote(here, there, *sems, devices[stage])

    def compute(place_):
        blocks = jnp.concatenate([mine[place_], theirs[place_]], axis=0)
        block_high, block_low = halves(blocks)
        total = narrow_dot(block_high, low[...], LAST) + narrow_dot(block_low, high[...], LAST)
        total = total + narrow_dot(block_high, high[...], LAST)
        for k, side in enumerate((lane, 1 - lane)):
            start = (place_ * SIDES + side) * share
            sums[0][pl.ds(pl.multiple_of(start, share), share), :] = total[k * share : (k + 1) * share]
        summing(0, place_).start()

    def step(stage, place_):
        summing(stage, place_).wait_recv()
        sums[stage + 1][unit(place_), :] = sums[stage][unit(place_), :] + landed[stage][unit(place_), :]
        if stage + 1 < stages:
            summing(stage + 1, place_).start()

    def progress(d):
        for stage in range(stages):
            for way in range(2):

                @pl.when(line.has(way, d - 1 - stage))
                def _():
                    step(stage, place + (d - 1 - stage) * (2 * way - 1))

    def half_rows(position):
        return pl.ds(pl.multiple_of(position * half, half), half)

    def scatter_b():
        return remote(part_b.at[half_rows(1 - part), :], land_b, b_s.at[0], b_r.at[0], {"col": twin})

    def exchange_b(stage):
        device = {"col": partner(col, bits[stage])}
        return remote(sums_b[stage - 1], landed_b[stage - 1], b_s.at[stage], b_r.at[stage], device)

    def return_b(position):
        rows = half_rows(position)
        index = len(bits)
        return remote(sums_b[-1], proj_b.at[rows, :], b_s.at[index], b_r.at[index], {"col": twin})

    def begin_b():
        small_local.wait()
        for k in range(1, row_count):
            small(k).wait_recv()
        flat = all_b[...].reshape(rank, basis_b.shape[1])
        part_b[...] = split_dot(flat, buffer_b[...], LAST)
        scatter_b().start()

    def second_b():
        scatter_b().wait_recv()
        sums_b[0][...] = part_b[half_rows(part), :] + land_b[...]
        if len(bits) > 1:
            exchange_b(1).start()

    def finish_b():
        for stage in range(1, len(bits)):
            exchange_b(stage).wait_recv()
            sums_b[stage][...] = sums_b[stage - 1][...] + landed_b[stage - 1][...]
            if stage + 1 < len(bits):
                exchange_b(stage + 1).start()
        return_b(part).start()
        proj_b[half_rows(part), :] = sums_b[-1][...]

    swap_basis.wait_recv()
    line.start(1)

    def advance(d, carry):
        line.forward(d)

        @pl.when(d == 1)
        def _():
            begin_b()
            own_basis.wait()
            own_rows.wait()
            swap_rows.wait_recv()
            high[...], low[...] = halves(pair[...].reshape(high.shape))
            compute(place)

        for way in range(2):

            @pl.when(line.has(way, d))
            def _():
                compute(place + d * (2 * way - 1))

        @pl.when(d == min(2, depth - 1))
        def _():
            second_b()

        progress(d)
        return carry

    lax.fori_loop(1, depth, advance, 0)
    finish_b()
    for d in range(depth, depth + stages):
        progress(d)
    return_b(1 - part).wait_recv()
    swap_basis.wait_send()
    swap_rows.wait_send()
    for k in range(1, row_count):
        small(k).wait_send()
    line.drain()

    def sent(place_, carry):
        for stage in range(stages):
            summing(stage, place_).wait_send()
        return carry

    lax.fori_loop(0, depth, sent, 0)
    scatter_b().wait_send()
    for stage in range(1, len(bits)):
        exchange_b(stage).wait_send()
    return_b(part).wait_send()


def project(basis_a, basis_b, buffer_a, buffer_b):
    row_count, col_count = lax.axis_size("row"), lax.axis_size("col")
    bits = col_bits(col_count)
    stages = len(bits) + 1
    depth = row_count // SIDES
    (share, width), rows_a, rows_b = basis_a.shape, buffer_a.shape[0], buffer_b.shape[0]
    rank, width = share * row_count, width // SIDES

    def space(*shape):
        return pltpu.VMEM(shape, jnp.float32)

    narrow = pltpu.VMEM((SIDES * rows_a, width), jnp.bfloat16)
    return pl.pallas_call(
        functools.partial(project_kernel, row_count, bits),
        out_shape=[
            jax.ShapeDtypeStruct(shape, jnp.float32)
            for shape in ((rank, SIDES * rows_a), (rank, rows_b), (SIDES, rows_a, width))
        ],
        in_specs=[VMEM] * 4,
        out_specs=[VMEM] * 3,
        scratch_shapes=[
            space(depth, share, width),
            space(depth, share, width),
            space(row_count, *basis_b.shape),
            narrow,
            narrow,
            space(rank, rows_b),
            space(rank // 2, rows_b),
        ]
        + [space(rank, SIDES * rows_a)] * (2 * stages)
        + [space(rank // 2, rows_b)] * (2 * len(bits) - 1)
        + Line.scratch(row_count, 2)
        + [DMA((row_count,)), DMA((row_count,)), DMA(()), DMA((2,)), DMA((2,)), DMA((2,))]
        + [DMA((stages, depth))] * 2
        + [DMA((len(bits) + 1,))] * 2,
        name="project",
        compiler_params=pltpu.CompilerParams(
            collective_id=1, has_side_effects=True, vmem_limit_bytes=60 * 2**20
        ),
    )(basis_a, basis_b, buffer_a, buffer_b)


def factor(rank, grams, outs, works, diags, between):
    eye_rows = lax.broadcasted_iota(jnp.int32, (rank, rank), 0)
    eye_cols = lax.broadcasted_iota(jnp.int32, (rank, rank), 1)
    for gram, work in zip(grams, works):
        work[:, :rank] = gram[...]
        work[:, rank:] = (eye_rows == eye_cols).astype(jnp.float32)
    rows = lax.broadcasted_iota(jnp.int32, (BLOCK, 1), 0)
    lanes = lax.broadcasted_iota(jnp.int32, (1, BLOCK), 1)
    for k in range(rank // BLOCK):
        low, high = k * BLOCK, (k + 1) * BLOCK
        for work, diag in zip(works, diags):
            diag[:, :BLOCK] = work[low:high, low:high]
            diag[:, BLOCK:] = (rows == lanes).astype(jnp.float32)

        def step(j, carry):
            for diag in diags:
                here = lanes == j
                row = diag[pl.ds(j, 1), :]
                col = jnp.sum(jnp.where(here, diag[:, :BLOCK], 0.0), axis=1, keepdims=True)
                pivot = jnp.sum(jnp.where(here, row[:, :BLOCK], 0.0), axis=1, keepdims=True)
                factor = jnp.where(rows > j, col * (1.0 / pivot), 0.0)
                diag[...] = diag[...] - factor * row
            return carry

        for piece in range(PIECES):
            lax.fori_loop(piece * BLOCK // PIECES, (piece + 1) * BLOCK // PIECES, step, 0)
            if piece + 1 < PIECES:
                between()
        width = slice(low, rank + high)
        for work, diag in zip(works, diags):
            pivots = jnp.sum(
                jnp.where(rows == lanes, diag[:, :BLOCK], 0.0), axis=1, keepdims=True
            )
            inverse = diag[:, BLOCK:] * (1.0 / jnp.sqrt(pivots))
            panel = dot(inverse, work[low:high, width])
            work[low:high, width] = panel
            if high < rank:
                factors = panel[:, BLOCK : rank - low]
                work[high:, width] = work[high:, width] - dot(factors, panel, FIRST)
        between()
    for work, out in zip(works, outs):
        out[...] = work[:, rank:]


class Reduce:
    def __init__(self, row_count, sems):
        depth = row_count // SIDES
        row = lax.axis_index("row")
        place, lane = row // SIDES, lax.rem(row, SIDES)
        lower = place < depth // 2
        self.place, self.lane, self.depth = place, lane, depth
        self.other = place * SIDES + (1 - lane)
        toward = jnp.where(lower, SIDES, -SIDES)
        self.inner, self.outer = {"row": row + toward}, {"row": row - toward}
        self.steps = jnp.where(lower, depth // 2 - 1 - place, place - depth // 2)
        self.middle = self.steps == 0
        self.has_outer = self.steps < depth // 2 - 1
        self.sems = sems

    @staticmethod
    def scratch(count):
        return [DMA((count,))] * 6

    def inward(self, i, part, arrive):
        return remote(part, arrive, self.sems[0].at[i], self.sems[1].at[i], self.inner)

    def swap(self, i, part, meet):
        return remote(part, meet, self.sems[2].at[i], self.sems[3].at[i], self.inner)

    def outward(self, i, final):
        return remote(final, final, self.sems[4].at[i], self.sems[5].at[i], self.outer)

    def gather(self, i, part, arrive, meet):
        @pl.when(self.has_outer)
        def _():
            self.inward(i, part, arrive).wait_recv()
            part[...] = part[...] + arrive[...]

        @pl.when(self.middle)
        def _():
            self.swap(i, part, meet).start()

        @pl.when(self.steps > 0)
        def _():
            self.inward(i, part, arrive).start()

    def spread(self, i, part, meet, final):
        @pl.when(self.middle)
        def _():
            self.swap(i, part, meet).wait_recv()
            final[...] = part[...] + meet[...]

        @pl.when(self.steps > 0)
        def _():
            self.outward(i, final).wait_recv()

        @pl.when(self.has_outer)
        def _():
            self.outward(i, final).start()

    def drain(self, i, part, arrive, meet, final):
        @pl.when(self.middle)
        def _():
            self.swap(i, part, meet).wait_send()

        @pl.when(self.steps > 0)
        def _():
            self.inward(i, part, arrive).wait_send()

        @pl.when(self.has_outer)
        def _():
            self.outward(i, final).wait_send()


def products_kernel(row_count, col_count, rank, scales, *refs):
    proj_a, proj_b, pair, buffer_b = refs[:4]
    trans_a, trans_b, basis_a, basis_b, ortho_a, ortho_b, scaled_a, scaled_b = refs[4:12]
    part_w, arrive_w, meet_w, final_w, other_w = refs[12:17]
    part_v, arrive_v, meet_v, final_v, land_v, other_v, whole_v = refs[17:24]
    piece_a, piece_b = refs[24:28], refs[28:32]
    cast_b, land_b, gram_a, gram_b, inv_a, inv_b, high_a, low_a = refs[32:40]
    rows_a, wide_a, wide_b, full_a, full_b, square_a, square_b, mine, theirs = refs[40:49]
    works, diags = refs[49:51], refs[51:53]
    reduce_sems, refs = refs[53:59], refs[59:]
    side_s, side_r, give_s, give_r, gram_s, gram_r, sq_s, sq_r = refs
    row, col = lax.axis_index("row"), lax.axis_index("col")
    line = Reduce(row_count, reduce_sems)
    lane, place, other = line.lane, line.place, line.other
    share, half = rank // row_count, rank // 2
    peers = SIDES * col_count
    piece = rank // peers
    index = lane * col_count + col
    chunks = part_w.shape[0]
    width = part_w.shape[2]

    def peer_of(k):
        target = lax.rem(index + k, peers)
        return (place * SIDES + target // col_count, lax.rem(target, col_count))

    barrier = pltpu.get_barrier_semaphore()

    pl.semaphore_signal(barrier, inc=1, device_id=line.inner, device_id_type=MESH)
    for k in range(1, peers):
        pl.semaphore_signal(barrier, inc=1, device_id=peer_of(k), device_id_type=MESH)

    @pl.when(line.has_outer)
    def _():
        pl.semaphore_signal(barrier, inc=1, device_id=line.outer, device_id_type=MESH)
        pl.semaphore_wait(barrier, peers + 1)

    @pl.when(jnp.logical_not(line.has_outer))
    def _():
        pl.semaphore_wait(barrier, peers)

    def rows_of(position, size):
        return pl.ds(pl.multiple_of(position * size, size), size)

    def give_g():
        return remote(cast_b, land_b, give_s.at[0], give_r.at[0], {"row": other})

    def give_v():
        there = whole_v.at[rows_of(1 - lane, half), :]
        return remote(there, land_v, give_s.at[1], give_r.at[1], {"row": other})

    def grams(k, which):
        source = (piece_a, piece_b)[which][3]
        target = (gram_a, gram_b)[which].at[rows_of(index, piece), :]
        return remote(source, target, gram_s.at[which, k], gram_r.at[which, k], peer_of(k))

    def aside(i, final, target):
        return remote(final, target, side_s.at[i], side_r.at[i], {"row": other})

    unit_v = (part_v, arrive_v, meet_v, final_v)

    def unit_w(k):
        return part_w.at[k], arrive_w.at[k], meet_w.at[k], final_w.at[k]

    def gather(i, unit):
        line.gather(i, unit[0], unit[1], unit[2])

    def spread(i, unit):
        line.spread(i, unit[0], unit[2], unit[3])

    theirs_index = (1 - lane) * col_count + col
    cast_b[...] = dot(proj_b[rows_of(theirs_index, piece), :], proj_b[...], LAST)
    give_g().start()
    piece_a[0][...] = dot(proj_a[rows_of(index, piece), :], proj_a[...], LAST)
    gather(0, piece_a)
    piece_b[0][...] = dot(proj_b[rows_of(index, piece), :], proj_b[...], LAST)
    give_g().wait_recv()
    piece_b[0][...] = piece_b[0][...] + land_b[...]
    gather(1, piece_b)
    rows_high, rows_low = halves(proj_a[...])

    def multiply(k):
        columns = slice(k * width, (k + 1) * width)
        block = pair[:, :, columns].reshape(proj_a.shape[1], width)
        block_high, block_low = halves(block)
        total = narrow_dot(rows_high, block_low) + narrow_dot(rows_low, block_high)
        part_w[k] = total + narrow_dot(rows_high, block_high)

    def take(k):
        gather(3 + k, unit_w(k))

    def hand(k):
        spread(3 + k, unit_w(k))
        aside(1 + k, final_w.at[k], other_w.at[k]).start()

    def take_v():
        give_v().wait_recv()
        part_v[...] = whole_v[rows_of(lane, half), :] + land_v[...]
        gather(2, unit_v)

    def hand_v():
        spread(2, unit_v)
        aside(0, final_v, other_v).start()

    multiply(0)
    for which, unit in enumerate((piece_a, piece_b)):
        spread(which, unit)
        for k in range(1, peers):
            grams(k, which).start()
    gram_a[rows_of(index, piece), :] = piece_a[3][...]
    gram_b[rows_of(index, piece), :] = piece_b[3][...]
    take(0)
    whole_v[...] = split_dot(proj_b[...], buffer_b[...])
    give_v().start()
    for k in range(1, chunks):
        multiply(k)

        @pl.when(jnp.logical_not(line.has_outer))
        def _():
            take(k)

    for which in range(2):
        for k in range(1, peers):
            grams(k, which).wait_recv()

    def later_take(k):
        @pl.when(line.has_outer)
        def _():
            take(k)

    tasks = [functools.partial(hand, 0), take_v]
    for k in range(1, chunks):
        tasks.append(functools.partial(later_take, k))
        if k == 2 or (chunks <= 2 and k == chunks - 1):
            tasks.append(hand_v)
        tasks.append(functools.partial(hand, k))
    if chunks == 1:
        tasks.append(hand_v)
    slots = rank // BLOCK * PIECES
    done = [0, 0]

    def between():
        done[0] += 1
        goal = -(-len(tasks) * done[0] // slots)
        while done[1] < min(goal, len(tasks)):
            tasks[done[1]]()
            done[1] += 1

    factor(rank, [gram_a, gram_b], [inv_a, inv_b], works, diags, between)
    high_a[...], low_a[...] = halves(inv_a[...])
    rows_a[...] = proj_a[...].T
    count_a = rows_a.shape[0] // SIDES
    wide_a[...] = split_dot(rows_a[rows_of(lane, count_a), :], inv_a[...], LAST)
    wide_b[...] = split_dot(proj_b[...].T, inv_b[...], LAST)
    ortho_a[...] = wide_a[...].astype(jnp.bfloat16)
    ortho_b[...] = wide_b[...].astype(jnp.bfloat16)
    square_a[...] = jnp.zeros_like(square_a)
    own = rows_of(row, share)

    def use(product, position):
        product_high, product_low = halves(product)
        total = narrow_dot(high_a[...], product_low) + narrow_dot(low_a[...], product_high)
        total = total + narrow_dot(high_a[...], product_high)
        full_a[...] = total
        trans_a[position] = total.astype(jnp.bfloat16)
        square_a[...] += jnp.sum(total * total, axis=1, keepdims=True)
        basis_a[position] = full_a[own, :]

    def near(k, carry):
        use(final_w[k], lane * chunks + k)
        return carry

    def far(k, carry):
        aside(1 + k, final_w.at[k], other_w.at[k]).wait_recv()
        use(other_w[k], (1 - lane) * chunks + k)
        return carry

    lax.fori_loop(0, chunks, near, 0)
    aside(0, final_v, other_v).wait_recv()
    whole_v[rows_of(lane, half), :] = final_v[...]
    give_v().wait_send()
    whole_v[rows_of(1 - lane, half), :] = other_v[...]
    total_b = split_dot(inv_b[...], whole_v[...])
    full_b[...] = total_b
    trans_b[...] = total_b.astype(jnp.bfloat16)
    square_b[...] = jnp.sum(total_b * total_b, axis=1, keepdims=True)
    lax.fori_loop(0, chunks, far, 0)

    def across(column):
        return jnp.broadcast_to(column, (rank, BLOCK)).T[:8]

    def norms(k):
        peer = lax.rem(col + k, col_count)
        return remote(mine, theirs.at[col], sq_s.at[k], sq_r.at[k], {"col": peer})

    mine[0] = across(square_a[...])
    mine[1] = across(square_b[...])
    for k in range(1, col_count):
        norms(k).start()
    theirs[col] = mine[...]
    for k in range(1, col_count):
        norms(k).wait_recv()
    norm = jnp.sqrt(jnp.sum(theirs[...], axis=0) + EPS)
    norm_a, norm_b = norm[0, :1], norm[1, :1]
    scaled_a[...] = (wide_a[...] * (scales[0] / norm_a)).astype(jnp.bfloat16)
    scaled_b[...] = (wide_b[...] * (scales[1] / norm_b)).astype(jnp.bfloat16)
    ranks = lax.broadcasted_iota(jnp.int32, (share, rank), 1)
    owned = lax.broadcasted_iota(jnp.int32, (share, rank), 0) + row * share
    own_a = jnp.sum(jnp.where(ranks == owned, norm_a, 0.0), axis=1, keepdims=True)
    own_b = jnp.sum(jnp.where(ranks == owned, norm_b, 0.0), axis=1, keepdims=True)
    for k in range(basis_a.shape[0]):
        basis_a[k] = basis_a[k] / own_a
    basis_b[...] = full_b[own, :] / own_b
    for k in range(1, col_count):
        norms(k).wait_send()
    for which in range(2):
        for k in range(1, peers):
            grams(k, which).wait_send()
    give_g().wait_send()
    aside(0, final_v, other_v).wait_send()
    for i, unit in enumerate((piece_a, piece_b, unit_v)):
        line.drain(i, *unit)

    def sent(k, carry):
        aside(1 + k, final_w.at[k], other_w.at[k]).wait_send()
        line.drain(3 + k, *unit_w(k))
        return carry

    lax.fori_loop(0, chunks, sent, 0)


def products(proj_a, proj_b, pair, buffer_b, scales):
    row_count, col_count = lax.axis_size("row"), lax.axis_size("col")
    rank = proj_a.shape[0]
    share, half, piece = rank // row_count, rank // 2, rank // (SIDES * col_count)
    side_width = pair.shape[2]
    chunk = CHUNK if side_width % CHUNK == 0 else side_width
    chunks = side_width // chunk
    width_b = buffer_b.shape[1]
    rows_a, rows_b = pair.shape[1], buffer_b.shape[0]

    def array(kind, *shape):
        return jax.ShapeDtypeStruct(shape, kind)

    def space(*shape):
        return pltpu.VMEM(shape, jnp.float32)

    narrow, wide = jnp.bfloat16, jnp.float32
    peers, cols = DMA((2, SIDES * col_count)), DMA((col_count,))
    return pl.pallas_call(
        functools.partial(products_kernel, row_count, col_count, rank, scales),
        out_shape=[
            array(narrow, SIDES * chunks, rank, chunk),
            array(narrow, rank, width_b),
            array(wide, SIDES * chunks, share, chunk),
            array(wide, share, width_b),
            array(narrow, rows_a, rank),
            array(narrow, rows_b, rank),
            array(narrow, rows_a, rank),
            array(narrow, rows_b, rank),
        ],
        in_specs=[VMEM] * 4,
        out_specs=[VMEM] * 8,
        scratch_shapes=[space(chunks, rank, chunk)] * 5
        + [space(half, width_b)] * 6
        + [space(rank, width_b)]
        + [space(piece, rank)] * 10
        + [space(rank, rank)] * 4
        + [pltpu.VMEM((rank, rank), narrow)] * 2
        + [
            space(SIDES * rows_a, rank),
            space(rows_a, rank),
            space(rows_b, rank),
            space(rank, chunk),
            space(rank, width_b),
            space(rank, 1),
            space(rank, 1),
            space(2, 8, rank),
            space(col_count, 2, 8, rank),
        ]
        + [space(rank, 2 * rank)] * 2
        + [space(BLOCK, 2 * BLOCK)] * 2
        + Reduce.scratch(3 + chunks)
        + [DMA((1 + chunks,))] * 2
        + [DMA((2,))] * 2
        + [peers, peers, cols, cols],
        name="products",
        compiler_params=pltpu.CompilerParams(
            collective_id=2, has_side_effects=True, vmem_limit_bytes=62 * 2**20
        ),
    )(proj_a, proj_b, pair, buffer_b)


def ending_kernel(slabs, *refs):
    buffer_a, trans_a, basis_a, ortho_a, scaled_a = refs[:5]
    buffer_b, trans_b, ortho_b, scaled_b = refs[5:9]
    mom_a, update_a, new_a, mom_b, update_b = refs[9:]
    mom_a[...] = buffer_a[...] - (1.0 - MU) * narrow_dot(ortho_a[...], trans_a[0])
    update_a[...] = narrow_dot(scaled_a[...], trans_a[0]).astype(jnp.bfloat16)
    new_a[...] = basis_a[0]

    @pl.when(pl.program_id(0) < slabs)
    def _():
        mom_b[...] = buffer_b[...] - (1.0 - MU) * narrow_dot(ortho_b[...], trans_b[...])
        update_b[...] = narrow_dot(scaled_b[...], trans_b[...]).astype(jnp.bfloat16)


def ending(buffer_a, trans_a, basis_a, ortho_a, scaled_a, buffer_b, trans_b, ortho_b, scaled_b):
    steps, rank, width = trans_a.shape
    rows_a, rows_b, share = buffer_a.shape[0], buffer_b.shape[0], basis_a.shape[1]
    slabs = 8
    if width % 128 or rows_b % (16 * slabs) or steps < slabs:
        flat = trans_a.swapaxes(0, 1).reshape(rank, -1)
        return (
            buffer_a - (1.0 - MU) * narrow_dot(ortho_a, flat),
            narrow_dot(scaled_a, flat).astype(jnp.bfloat16),
            basis_a.swapaxes(0, 1).reshape(share, -1),
            buffer_b - (1.0 - MU) * narrow_dot(ortho_b, trans_b),
            narrow_dot(scaled_b, trans_b).astype(jnp.bfloat16),
        )
    some = rows_b // slabs
    cut = pl.BlockSpec((rows_a, width), lambda j: (0, j))
    stack = pl.BlockSpec((1, rank, width), lambda j: (j, 0, 0))
    thin = pl.BlockSpec((1, share, width), lambda j: (j, 0, 0))
    fixed_a = pl.BlockSpec((rows_a, rank), lambda j: (0, 0))
    fixed_b = pl.BlockSpec(trans_b.shape, lambda j: (0, 0))
    slab = pl.BlockSpec((some, buffer_b.shape[1]), lambda j: (jnp.minimum(j, slabs - 1), 0))
    rows = pl.BlockSpec((some, rank), lambda j: (jnp.minimum(j, slabs - 1), 0))
    return pl.pallas_call(
        functools.partial(ending_kernel, slabs),
        grid=(steps,),
        out_shape=[
            jax.ShapeDtypeStruct(buffer_a.shape, jnp.float32),
            jax.ShapeDtypeStruct(buffer_a.shape, jnp.bfloat16),
            jax.ShapeDtypeStruct((share, buffer_a.shape[1]), jnp.float32),
            jax.ShapeDtypeStruct(buffer_b.shape, jnp.float32),
            jax.ShapeDtypeStruct(buffer_b.shape, jnp.bfloat16),
        ],
        in_specs=[cut, stack, thin, fixed_a, fixed_a, slab, fixed_b, rows, rows],
        out_specs=[cut, cut, pl.BlockSpec((share, width), lambda j: (0, j)), slab, slab],
        name="ending",
    )(buffer_a, trans_a, basis_a, ortho_a, scaled_a, buffer_b, trans_b, ortho_b, scaled_b)


def shards(mom_a, grad_a, basis_a, mom_b, grad_b, basis_b):
    row_count = lax.axis_size("row")
    buffer_a, buffer_b = MU * mom_a + grad_a, MU * mom_b + grad_b
    proj_a, proj_b, pair = project(basis_a, basis_b, buffer_a, buffer_b)
    rank = proj_a.shape[0]
    scales = [
        math.sqrt(x.shape[0] * x.shape[1] * row_count * lax.axis_size("col") / rank)
        for x in (buffer_a, buffer_b)
    ]
    trans_a, trans_b, basis_a, basis_b, ortho_a, ortho_b, scaled_a, scaled_b = products(
        proj_a, proj_b, pair, buffer_b, scales
    )
    new_mom_a, update_a, new_basis_a, new_mom_b, update_b = ending(
        buffer_a, trans_a, basis_a, ortho_a, scaled_a, buffer_b, trans_b, ortho_b, scaled_b
    )
    return new_mom_a, update_a, new_basis_a, new_mom_b, update_b, basis_b


def solution(mesh):
    spec = P("row", "col")
    return jax.shard_map(
        shards, mesh=mesh, in_specs=(spec,) * 6, out_specs=(spec,) * 6, check_vma=False
    )
```

time: 510 us -> 342 us (0.67)
  Pallas kernels: 68.2 us -> 333 us
  waiting for transfers between devices: 262 us -> 0 us
  matrix products: 78.7 us -> 0 us
  blocking collectives: 53.9 us -> 0 us
  between operations: 14.5 us -> 0.67 us
  local copies, waits for them, and re-layouts: 10.3 us -> 0.65 us
  starting transfers between devices: 5.27 us -> 0 us
  other arithmetic: 11.7 us -> 6.58 us
    pallas_call x1 -> x3, Pallas kernels: 68.2 us -> 333 us  [the longest x1 218 us: products(): pl.pallas_call(functools.partial(products_kernel, row_count, col_count, r...]
    all_gather x3 -> x0, waiting for transfers between devices: 204 us -> none  [the longest x1 110 us: shards(): lax.all_gather(jnp.concatenate([basis_a, basis_b], axis=1), 'row', axis=0...]
    dot_general x14 -> x0, matrix products: 78.7 us -> none  [dot(): lax.dot_general(x, y, (contract, ((), ())), precision=HIGHEST, preferred_...]
    psum x1 -> x0, waiting for transfers between devices: 57.7 us -> none  [shards(): proj_a, proj_b = lax.psum((partial_a, partial_b), 'col')]
    all_to_all x1 -> x0, blocking collectives: 48 us -> none  [reduce_rows(): return jnp.sum(lax.all_to_all(shares, 'row', 0, 0), axis=0)]
    psum x1 -> x0, blocking collectives: 5.89 us -> none  [shards(): lax.psum((jnp.sum(trans_a * trans_a, axis=1, keepdims=True), jnp.sum(tran...]
    concatenate x4 -> x0, other arithmetic: 5.18 us -> none  [the longest x1 2.16 us: shards(): jnp.concatenate([basis_a, basis_b], axis=1)]
  transfers between devices with their start and end apart: 5 -> 0, of which waited for: 4 -> 0; matrix products, arithmetic and copies ran while one was open for 4% -> 0% of each run, Pallas kernels for 14% -> 0%
where the time goes in v2:
time: 342 us; the launch traced here: 341 us
  Pallas kernels  333 us (97%)
  other arithmetic  6.58 us (2%)
    pallas_call x1, Pallas kernels, products(): pl.pallas_call(functools.partial(products_kernel, row_count, col_count, r...  218 us
    pallas_call x1, Pallas kernels, project(): pl.pallas_call(functools.partial(project_kernel, row_count, bits), out_sh...  103 us
    pallas_call x1, Pallas kernels, ending(): pl.pallas_call(functools.partial(ending_kernel, slabs), grid=(steps,), ou...  12.6 us

profile of v2, /device:TPU:0, one launch (start us, length us, event | category | flops | bytes accessed | tf_op | source)
XLA Modules:
  0.0 341.1 jit_solution(15992340323780691724)
XLA Ops:
  0.6 0.0 copy-start
  0.6 3.2 multiply_add_fusion.1.refs_3_.refs_5_
  3.8 0.0 copy-done
  3.8 3.4 %multiply_add_fusion.refs_2_.refs_0_ = f32[192,3072]{1,0:T(8,128)} fusion(f32[192,3072]{1,0:T(8,128)S(1)} %copy-done, f32[192,3072]{1,0:T(8,128)} %param.6), kind=kLoop, calls=%fused_computation | loop fusion | flops 1179648 | bytes 7077888 | tf_op jit(solution)/shard_map/add | solution.py:830
  7.2 102.6 %project.1 = (f32[512,384]{1,0:T(8,128)}, f32[512,896]{1,0:T(8,128)}, f32[2,192,1536]{2,1,0:T(8,128)}) custom-call(f32[64,3072]{1,0:T(8,128)} %refs_0_.1, f32[64,384]{1,0:T(8,128)} %refs_1_.1, f32[192,3072]{1,0:T(8,128)} %multiply_add_fusion.refs_2_.refs_0_, f32[896,384]{1,0:T(8,128)} %multiply_add_fusion.1.refs_3_.refs_5_), custom_call_target="tpu_custom_call" | custom-call | tf_op jit(solution)/shard_map/project/pallas_call | solution.py:341
  109.8 218.0 %products.1 = (bf16[12,512,256]{2,1,0:T(8,128)(2,1)}, bf16[512,384]{1,0:T(8,128)(2,1)}, f32[12,64,256]{2,1,0:T(8,128)}, f32[64,384]{1,0:T(8,128)}, bf16[192,512]...) custom-call(f32[512,384]{1,0:T(8,128)} %get-tuple-element.22.refs_0_, ...), custom_call_target="tpu_custom_call" | custom-call | tf_op jit(solution)/shard_map/products/pallas_call | solution.py:733
  327.9 0.0 copy-start.1
  327.9 12.6 %ending.1 = (f32[192,3072]{1,0:T(8,128)}, bf16[192,3072]{1,0:T(8,128)(2,1)}, f32[64,3072]{1,0:T(8,128)}, f32[896,384]{1,0:T(8,128)}, bf16[896,384]{1,0:T(8,128)(2,1)}) custom-call(f32[192,3072]{1,0:T(8,128)} %multiply_add_fusion.refs_2_.refs_0_, bf16[12,512,256]{2,1,0:T(8,128)(2,1)} %get-tuple-element.25.refs_1_, f32[12,64,256]{2,1,0:T(8,128)} %get-tuple-element.26.refs_2_, ...), custom_call_target="tpu_custom_call" | custom-call | tf_op jit(solution)/shard_map/ending/pallas_call | solution.py:812
  340.5 0.0 copy-done.1
  340.5 0.6 copy.13
Async XLA Ops:
  0.6 3.2 copy-start
  327.9 12.6 %copy-start.1 = (f32[64,384]{1,0:T(8,128)S(1)}, f32[64,384]{1,0:T(8,128)}, u32[]{:S(2)}) copy-start(f32[64,384]{1,0:T(8,128)} %get-tuple-element.49) | copy-start | bytes 294916

commit v3 on v2

--- a/solution.py
+++ b/solution.py
@@ -20,7 +20,7 @@
 PLAIN = ((1,), (0,))
 SIDES = 2
 PIECES = 2
-CHUNK = 256
+CHUNK = 128
 
 
 def dot(x, y, contract=PLAIN, precision=HIGHEST):
@@ -482,7 +482,7 @@
             self.outward(i, final).wait_send()
 
 
-def products_kernel(row_count, col_count, rank, scales, *refs):
+def products_kernel(row_count, col_count, rank, joined, scales, *refs):
     proj_a, proj_b, pair, buffer_b = refs[:4]
     trans_a, trans_b, basis_a, basis_b, ortho_a, ortho_b, scaled_a, scaled_b = refs[4:12]
     part_w, arrive_w, meet_w, final_w, other_w = refs[12:17]
@@ -585,40 +585,61 @@
         spread(2, unit_v)
         aside(0, final_v, other_v).start()
 
+    def later_take(k):
+        @pl.when(line.has_outer)
+        def _():
+            take(k)
+
+    def later_take_v():
+        @pl.when(line.has_outer)
+        def _():
+            take_v()
+
+    early = jnp.logical_not(line.has_outer)
     multiply(0)
+
+    @pl.when(early)
+    def _():
+        take(0)
+
     for which, unit in enumerate((piece_a, piece_b)):
         spread(which, unit)
         for k in range(1, peers):
             grams(k, which).start()
     gram_a[rows_of(index, piece), :] = piece_a[3][...]
     gram_b[rows_of(index, piece), :] = piece_b[3][...]
-    take(0)
     whole_v[...] = split_dot(proj_b[...], buffer_b[...])
     give_v().start()
     for k in range(1, chunks):
         multiply(k)
 
-        @pl.when(jnp.logical_not(line.has_outer))
+        @pl.when(early)
         def _():
             take(k)
 
+        if k == min(2, chunks - 1):
+
+            @pl.when(early)
+            def _():
+                take_v()
+
+    tasks = []
+    for k in range(chunks):
+        tasks.append(functools.partial(later_take, k))
+        if k > 0:
+            tasks.append(functools.partial(hand, k - 1))
+        if k == min(2, chunks - 1):
+            tasks.append(later_take_v)
+        if k == min(3, chunks - 1):
+            tasks.append(hand_v)
+    tasks.append(functools.partial(hand, chunks - 1))
+    first = min(4, len(tasks))
+    for task in tasks[:first]:
+        task()
+    tasks = tasks[first:]
     for which in range(2):
         for k in range(1, peers):
             grams(k, which).wait_recv()
-
-    def later_take(k):
-        @pl.when(line.has_outer)
-        def _():
-            take(k)
-
-    tasks = [functools.partial(hand, 0), take_v]
-    for k in range(1, chunks):
-        tasks.append(functools.partial(later_take, k))
-        if k == 2 or (chunks <= 2 and k == chunks - 1):
-            tasks.append(hand_v)
-        tasks.append(functools.partial(hand, k))
-    if chunks == 1:
-        tasks.append(hand_v)
     slots = rank // BLOCK * PIECES
     done = [0, 0]
 
@@ -649,16 +670,23 @@
         square_a[...] += jnp.sum(total * total, axis=1, keepdims=True)
         basis_a[position] = full_a[own, :]
 
+    groups = chunks // joined
+
+    def group(source, k):
+        return jnp.concatenate([source[k * joined + i] for i in range(joined)], axis=1)
+
     def near(k, carry):
-        use(final_w[k], lane * chunks + k)
+        use(group(final_w, k), lane * groups + k)
         return carry
 
     def far(k, carry):
-        aside(1 + k, final_w.at[k], other_w.at[k]).wait_recv()
-        use(other_w[k], (1 - lane) * chunks + k)
+        for i in range(joined):
+            j = k * joined + i
+            aside(1 + j, final_w.at[j], other_w.at[j]).wait_recv()
+        use(group(other_w, k), (1 - lane) * groups + k)
         return carry
 
-    lax.fori_loop(0, chunks, near, 0)
+    lax.fori_loop(0, groups, near, 0)
     aside(0, final_v, other_v).wait_recv()
     whole_v[rows_of(lane, half), :] = final_v[...]
     give_v().wait_send()
@@ -667,7 +695,7 @@
     full_b[...] = total_b
     trans_b[...] = total_b.astype(jnp.bfloat16)
     square_b[...] = jnp.sum(total_b * total_b, axis=1, keepdims=True)
-    lax.fori_loop(0, chunks, far, 0)
+    lax.fori_loop(0, groups, far, 0)
 
     def across(column):
         return jnp.broadcast_to(column, (rank, BLOCK)).T[:8]
@@ -719,6 +747,8 @@
     side_width = pair.shape[2]
     chunk = CHUNK if side_width % CHUNK == 0 else side_width
     chunks = side_width // chunk
+    joined = 2 if chunks % 2 == 0 else 1
+    groups, wide_chunk = chunks // joined, chunk * joined
     width_b = buffer_b.shape[1]
     rows_a, rows_b = pair.shape[1], buffer_b.shape[0]
 
@@ -731,11 +761,11 @@
     narrow, wide = jnp.bfloat16, jnp.float32
     peers, cols = DMA((2, SIDES * col_count)), DMA((col_count,))
     return pl.pallas_call(
-        functools.partial(products_kernel, row_count, col_count, rank, scales),
+        functools.partial(products_kernel, row_count, col_count, rank, joined, scales),
         out_shape=[
-            array(narrow, SIDES * chunks, rank, chunk),
+            array(narrow, SIDES * groups, rank, wide_chunk),
             array(narrow, rank, width_b),
-            array(wide, SIDES * chunks, share, chunk),
+            array(wide, SIDES * groups, share, wide_chunk),
             array(wide, share, width_b),
             array(narrow, rows_a, rank),
             array(narrow, rows_b, rank),
@@ -754,7 +784,7 @@
             space(SIDES * rows_a, rank),
             space(rows_a, rank),
             space(rows_b, rank),
-            space(rank, chunk),
+            space(rank, wide_chunk),
             space(rank, width_b),
             space(rank, 1),
             space(rank, 1),

time: 342 us -> 285 us (0.83)
  Pallas kernels: 333 us -> 276 us
    pallas_call x1, Pallas kernels: 218 us -> 161 us  [products(): pl.pallas_call(functools.partial(products_kernel, row_count, col_count, r...]
where the time goes in v3:
time: 285 us; the launch traced here: 284 us
  Pallas kernels  276 us (97%)
  other arithmetic  6.58 us (2%)
    pallas_call x1, Pallas kernels, products(): pl.pallas_call(functools.partial(products_kernel, row_count, col_count, r...  161 us
    pallas_call x1, Pallas kernels, project(): pl.pallas_call(functools.partial(project_kernel, row_count, bits), out_sh...  103 us
    pallas_call x1, Pallas kernels, ending(): pl.pallas_call(functools.partial(ending_kernel, slabs), grid=(steps,), ou...  12.6 us
    add x2, other arithmetic, shards(): buffer_a, buffer_b = (MU * mom_a + grad_a, MU * mom_b + grad_b)  6.58 us

profile of v3, /device:TPU:0, one launch (start us, length us, event | category | flops | bytes accessed | tf_op | source)
XLA Modules:
  0.0 284.1 jit_solution(10248603068287119168)
XLA Ops:
  0.6 0.0 copy-start
  0.6 3.2 %multiply_add_fusion.1.refs_3_.refs_5_ = f32[896,384]{1,0:T(8,128)} fusion(f32[896,384]{1,0:T(8,128)} %param.10, f32[896,384]{1,0:T(8,128)} %param.9), kind=kLoop, calls=%fused_computation.1 | loop fusion | flops 688128 | bytes 4128768 | tf_op jit(solution)/shard_map/add | solution.py:860
  3.8 0.0 copy-done
  3.8 3.4 %multiply_add_fusion.refs_2_.refs_0_ = f32[192,3072]{1,0:T(8,128)} fusion(f32[192,3072]{1,0:T(8,128)S(1)} %copy-done, f32[192,3072]{1,0:T(8,128)} %param.6), kind=kLoop, calls=%fused_computation | loop fusion | flops 1179648 | bytes 7077888 | tf_op jit(solution)/shard_map/add | solution.py:860
  7.2 102.6 %project.1 = (f32[512,384]{1,0:T(8,128)}, f32[512,896]{1,0:T(8,128)}, f32[2,192,1536]{2,1,0:T(8,128)}) custom-call(f32[64,3072]{1,0:T(8,128)} %refs_0_.1, f32[64,384]{1,0:T(8,128)} %refs_1_.1, f32[192,3072]{1,0:T(8,128)} %multiply_add_fusion.refs_2_.refs_0_, f32[896,384]{1,0:T(8,128)} %multiply_add_fusion.1.refs_3_.refs_5_), custom_call_target="tpu_custom_call" | custom-call | tf_op jit(solution)/shard_map/project/pallas_call | solution.py:341
  109.8 161.0 %products.1 = (bf16[12,512,256]{2,1,0:T(8,128)(2,1)}, bf16[512,384]{1,0:T(8,128)(2,1)}, f32[12,64,256]{2,1,0:T(8,128)}, f32[64,384]{1,0:T(8,128)}, bf16[192,512]...) custom-call(f32[512,384]{1,0:T(8,128)} %get-tuple-element.22.refs_0_, ...), custom_call_target="tpu_custom_call" | custom-call | tf_op jit(solution)/shard_map/products/pallas_call | solution.py:763
  270.8 0.0 copy-start.1
  270.8 12.6 %ending.1 = (f32[192,3072]{1,0:T(8,128)}, bf16[192,3072]{1,0:T(8,128)(2,1)}, f32[64,3072]{1,0:T(8,128)}, f32[896,384]{1,0:T(8,128)}, bf16[896,384]{1,0:T(8,128)(2,1)}) custom-call(f32[192,3072]{1,0:T(8,128)} %multiply_add_fusion.refs_2_.refs_0_, bf16[12,512,256]{2,1,0:T(8,128)(2,1)} %get-tuple-element.25.refs_1_, f32[12,64,256]{2,1,0:T(8,128)} %get-tuple-element.26.refs_2_, ...), custom_call_target="tpu_custom_call" | custom-call | tf_op jit(solution)/shard_map/ending/pallas_call | solution.py:842
  283.4 0.0 copy-done.1
  283.4 0.6 copy.13
Async XLA Ops:
  0.6 3.2 %copy-start = (f32[192,3072]{1,0:T(8,128)S(1)}, f32[192,3072]{1,0:T(8,128)}, u32[]{:S(2)}) copy-start(f32[192,3072]{1,0:T(8,128)} %param.7) | copy-start | bytes 7077892
  270.8 12.6 %copy-start.1 = (f32[64,384]{1,0:T(8,128)S(1)}, f32[64,384]{1,0:T(8,128)}, u32[]{:S(2)}) copy-start(f32[64,384]{1,0:T(8,128)} %get-tuple-element.49) | copy-start | bytes 294916

commit v4 on v3

--- a/solution.py
+++ b/solution.py
@@ -19,7 +19,8 @@
 FIRST = ((0,), (0,))
 PLAIN = ((1,), (0,))
 SIDES = 2
-PIECES = 2
+PIECES = 4
+PIVOTS = 4
 CHUNK = 128
 
 
@@ -182,8 +183,14 @@
         return pl.ds(pl.multiple_of(position * width, width), width)
 
     def small(k):
-        peer = lax.rem(row + k, row_count)
+        peer = lax.rem(place + k, depth) * SIDES + lane
         return remote(basis_b, all_b.at[row], small_s.at[k], small_r.at[k], {"row": peer})
+
+    def beside(k):
+        slot = lax.rem(place + depth - k, depth) * SIDES + lane
+        source = basis_b if k == 0 else all_b.at[slot]
+        sems = small_s.at[depth + k], small_r.at[depth + k]
+        return remote(source, all_b.at[slot], *sems, {"row": other})
 
     swap_basis = remote(
         basis_a.at[:, columns(1 - lane)], theirs.at[place], swap_s.at[0], swap_r.at[0], {"row": other}
@@ -198,20 +205,26 @@
     line = Line(row_count, sources, [mine, theirs], line_sems)
     swap_basis.start()
     line.start(0)
-    for k in range(1, row_count):
+    for k in range(1, depth):
         small(k).start()
+    beside(0).start()
     swap_rows.start()
     own_basis.start()
     own_rows.start()
     small_local.start()
 
-    def unit(place_):
-        return pl.ds(pl.multiple_of(place_ * SIDES * share, SIDES * share), SIDES * share)
+    def strip(place_, position):
+        return pl.ds(pl.multiple_of((place_ * SIDES + position) * share, share), share)
 
     def summing(stage, place_):
         sems = sum_s.at[stage, place_], sum_r.at[stage, place_]
-        here, there = sums[stage].at[unit(place_), :], landed[stage].at[unit(place_), :]
+        rows = strip(place_, part if stage else 1 - part)
+        here, there = sums[stage].at[rows, :], landed[stage].at[rows, :]
         return remote(here, there, *sems, devices[stage])
+
+    def giving(place_, position):
+        here = proj_a.at[strip(place_, position), :]
+        return remote(here, here, sum_s.at[stages, place_], sum_r.at[stages, place_], {"col": twin})
 
     def compute(place_):
         blocks = jnp.concatenate([mine[place_], theirs[place_]], axis=0)
@@ -225,17 +238,30 @@
 
     def step(stage, place_):
         summing(stage, place_).wait_recv()
-        sums[stage + 1][unit(place_), :] = sums[stage][unit(place_), :] + landed[stage][unit(place_), :]
+        rows = strip(place_, part)
+        sums[stage + 1][rows, :] = sums[stage][rows, :] + landed[stage][rows, :]
         if stage + 1 < stages:
             summing(stage + 1, place_).start()
-
-    def progress(d):
+        else:
+            giving(place_, part).start()
+
+    begin = min(2, depth - 1)
+
+    def progress(turn):
         for stage in range(stages):
+            d = turn - stage
+            for near in range(begin):
+                for way in range(2):
+
+                    @pl.when((d == begin) & line.has(way, near))
+                    def _():
+                        step(stage, place + near * (2 * way - 1))
+
             for way in range(2):
 
-                @pl.when(line.has(way, d - 1 - stage))
+                @pl.when((d >= begin) & line.has(way, d))
                 def _():
-                    step(stage, place + (d - 1 - stage) * (2 * way - 1))
+                    step(stage, place + d * (2 * way - 1))
 
     def half_rows(position):
         return pl.ds(pl.multiple_of(position * half, half), half)
@@ -252,10 +278,15 @@
         index = len(bits)
         return remote(sums_b[-1], proj_b.at[rows, :], b_s.at[index], b_r.at[index], {"col": twin})
 
+    def pass_b():
+        for k in range(1, depth):
+            small(k).wait_recv()
+            beside(k).start()
+
     def begin_b():
         small_local.wait()
-        for k in range(1, row_count):
-            small(k).wait_recv()
+        for k in range(depth):
+            beside(k).wait_recv()
         flat = all_b[...].reshape(rank, basis_b.shape[1])
         part_b[...] = split_dot(flat, buffer_b[...], LAST)
         scatter_b().start()
@@ -278,43 +309,57 @@
     swap_basis.wait_recv()
     line.start(1)
 
+    def units(d):
+        for way in range(2):
+
+            @pl.when(line.has(way, d))
+            def _():
+                compute(place + d * (2 * way - 1))
+
     def advance(d, carry):
         line.forward(d)
 
         @pl.when(d == 1)
         def _():
+            pass_b()
             begin_b()
+            if depth > 2:
+                second_b()
+
+        @pl.when(d == begin)
+        def _():
             own_basis.wait()
             own_rows.wait()
             swap_rows.wait_recv()
             high[...], low[...] = halves(pair[...].reshape(high.shape))
-            compute(place)
-
-        for way in range(2):
-
-            @pl.when(line.has(way, d))
-            def _():
-                compute(place + d * (2 * way - 1))
-
-        @pl.when(d == min(2, depth - 1))
-        def _():
-            second_b()
-
+            if depth == 2:
+                second_b()
+
+        def catch_up(near, inner):
+            units(near)
+            return inner
+
+        lax.fori_loop(jnp.where(d == begin, 0, d), jnp.where(d < begin, 0, d + 1), catch_up, 0)
         progress(d)
         return carry
 
     lax.fori_loop(1, depth, advance, 0)
+    progress(depth)
     finish_b()
-    for d in range(depth, depth + stages):
+    for d in range(depth + 1, depth + stages - 1):
         progress(d)
     return_b(1 - part).wait_recv()
     swap_basis.wait_send()
     swap_rows.wait_send()
-    for k in range(1, row_count):
+    for k in range(depth):
+        beside(k).wait_send()
+    for k in range(1, depth):
         small(k).wait_send()
     line.drain()
 
     def sent(place_, carry):
+        giving(place_, 1 - part).wait_recv()
+        giving(place_, part).wait_send()
         for stage in range(stages):
             summing(stage, place_).wait_send()
         return carry
@@ -359,7 +404,7 @@
         + [space(rank // 2, rows_b)] * (2 * len(bits) - 1)
         + Line.scratch(row_count, 2)
         + [DMA((row_count,)), DMA((row_count,)), DMA(()), DMA((2,)), DMA((2,)), DMA((2,))]
-        + [DMA((stages, depth))] * 2
+        + [DMA((stages + 1, depth))] * 2
         + [DMA((len(bits) + 1,))] * 2,
         name="project",
         compiler_params=pltpu.CompilerParams(
@@ -382,18 +427,35 @@
             diag[:, :BLOCK] = work[low:high, low:high]
             diag[:, BLOCK:] = (rows == lanes).astype(jnp.float32)
 
-        def step(j, carry):
+        def step(base, i, carry):
+            j = PIVOTS * i
             for diag in diags:
-                here = lanes == j
-                row = diag[pl.ds(j, 1), :]
-                col = jnp.sum(jnp.where(here, diag[:, :BLOCK], 0.0), axis=1, keepdims=True)
-                pivot = jnp.sum(jnp.where(here, row[:, :BLOCK], 0.0), axis=1, keepdims=True)
-                factor = jnp.where(rows > j, col * (1.0 / pivot), 0.0)
-                diag[...] = diag[...] - factor * row
+                square = diag[base:, :BLOCK]
+                tops = [diag[pl.ds(j + p, 1), :] for p in range(PIVOTS)]
+
+                def pick(some, p):
+                    kept = jnp.where(lanes == j + p, some[:, :BLOCK], 0.0)
+                    return jnp.sum(kept, axis=1, keepdims=True)
+
+                cols = [pick(square, p) for p in range(PIVOTS)]
+                cells = [[pick(top, p) for p in range(PIVOTS)] for top in tops]
+                total = diag[base:, :]
+                for p in range(PIVOTS):
+                    scale = 1.0 / cells[p][p]
+                    weights = jnp.where(rows[base:] > j + p, cols[p] * scale, 0.0)
+                    for q in range(p + 1, PIVOTS):
+                        ratio = cells[q][p] * scale
+                        tops[q] = tops[q] - ratio * tops[p]
+                        cols[q] = cols[q] - weights * cells[p][q]
+                        cells[q] = [cells[q][r] - ratio * cells[p][r] for r in range(PIVOTS)]
+                    total = total - weights * tops[p]
+                diag[base:, :] = total
             return carry
 
         for piece in range(PIECES):
-            lax.fori_loop(piece * BLOCK // PIECES, (piece + 1) * BLOCK // PIECES, step, 0)
+            steps = BLOCK // PIVOTS // PIECES
+            some = functools.partial(step, piece * BLOCK // PIECES)
+            lax.fori_loop(piece * steps, (piece + 1) * steps, some, 0)
             if piece + 1 < PIECES:
                 between()
         width = slice(low, rank + high)
@@ -532,10 +594,32 @@
         there = whole_v.at[rows_of(1 - lane, half), :]
         return remote(there, land_v, give_s.at[1], give_r.at[1], {"row": other})
 
-    def grams(k, which):
-        source = (piece_a, piece_b)[which][3]
-        target = (gram_a, gram_b)[which].at[rows_of(index, piece), :]
-        return remote(source, target, gram_s.at[which, k], gram_r.at[which, k], peer_of(k))
+    bits = col_bits(col_count)[::-1]
+
+    def held(stage):
+        columns = [col]
+        for bit in bits[: max(stage - 1, 0)]:
+            columns += [partner(c, bit) for c in columns]
+        sides = [lane] if stage == 0 else [lane, 1 - lane]
+        return [side * col_count + c for side in sides for c in columns]
+
+    def grams(stage):
+        device = {"row": other} if stage == 0 else {"col": partner(col, bits[stage - 1])}
+        copies = []
+        for k, position in enumerate(held(stage)):
+            for which, gram in enumerate((gram_a, gram_b)):
+                here = gram.at[rows_of(position, piece), :]
+                sems = gram_s.at[which, stage, k], gram_r.at[which, stage, k]
+                copies.append(remote(here, here, *sems, device))
+        return copies
+
+    def send_grams(stage):
+        for copy in grams(stage):
+            copy.start()
+
+    def await_grams(stage):
+        for copy in grams(stage):
+            copy.wait_recv()
 
     def aside(i, final, target):
         return remote(final, target, side_s.at[i], side_r.at[i], {"row": other})
@@ -604,10 +688,9 @@
 
     for which, unit in enumerate((piece_a, piece_b)):
         spread(which, unit)
-        for k in range(1, peers):
-            grams(k, which).start()
     gram_a[rows_of(index, piece), :] = piece_a[3][...]
     gram_b[rows_of(index, piece), :] = piece_b[3][...]
+    send_grams(0)
     whole_v[...] = split_dot(proj_b[...], buffer_b[...])
     give_v().start()
     for k in range(1, chunks):
@@ -623,23 +706,27 @@
             def _():
                 take_v()
 
+            await_grams(0)
+            send_grams(1)
+        if k == min(3, chunks - 1):
+            later_take(0)
+
     tasks = []
     for k in range(chunks):
-        tasks.append(functools.partial(later_take, k))
         if k > 0:
+            tasks.append(functools.partial(later_take, k))
             tasks.append(functools.partial(hand, k - 1))
         if k == min(2, chunks - 1):
             tasks.append(later_take_v)
         if k == min(3, chunks - 1):
             tasks.append(hand_v)
     tasks.append(functools.partial(hand, chunks - 1))
-    first = min(4, len(tasks))
-    for task in tasks[:first]:
-        task()
-    tasks = tasks[first:]
-    for which in range(2):
-        for k in range(1, peers):
-            grams(k, which).wait_recv()
+    for stage in range(1, len(bits) + 1):
+        for _ in range(min(2, len(tasks))):
+            tasks.pop(0)()
+        await_grams(stage)
+        if stage < len(bits):
+            send_grams(stage + 1)
     slots = rank // BLOCK * PIECES
     done = [0, 0]
 
@@ -724,9 +811,9 @@
     basis_b[...] = full_b[own, :] / own_b
     for k in range(1, col_count):
         norms(k).wait_send()
-    for which in range(2):
-        for k in range(1, peers):
-            grams(k, which).wait_send()
+    for stage in range(len(bits) + 1):
+        for copy in grams(stage):
+            copy.wait_send()
     give_g().wait_send()
     aside(0, final_v, other_v).wait_send()
     for i, unit in enumerate((piece_a, piece_b, unit_v)):
@@ -759,7 +846,8 @@
         return pltpu.VMEM(shape, jnp.float32)
 
     narrow, wide = jnp.bfloat16, jnp.float32
-    peers, cols = DMA((2, SIDES * col_count)), DMA((col_count,))
+    grams = DMA((2, len(col_bits(col_count)) + 1, SIDES * col_count))
+    cols = DMA((col_count,))
     return pl.pallas_call(
         functools.partial(products_kernel, row_count, col_count, rank, joined, scales),
         out_shape=[
@@ -796,7 +884,7 @@
         + Reduce.scratch(3 + chunks)
         + [DMA((1 + chunks,))] * 2
         + [DMA((2,))] * 2
-        + [peers, peers, cols, cols],
+        + [grams, grams, cols, cols],
         name="products",
         compiler_params=pltpu.CompilerParams(
             collective_id=2, has_side_effects=True, vmem_limit_bytes=62 * 2**20

time: 285 us -> 252 us (0.88)
  Pallas kernels: 276 us -> 244 us
    pallas_call x1, Pallas kernels: 161 us -> 138 us  [products(): pl.pallas_call(functools.partial(products_kernel, row_count, col_count, r...]
    pallas_call x1, Pallas kernels: 103 us -> 93.5 us  [project(): pl.pallas_call(functools.partial(project_kernel, row_count, bits), out_sh...]
where the time goes in v4:
time: 252 us
  Pallas kernels  244 us (97%)
  other arithmetic  6.58 us (3%)
    pallas_call x1, Pallas kernels, products(): pl.pallas_call(functools.partial(products_kernel, row_count, col_count, r...  138 us
    pallas_call x1, Pallas kernels, project(): pl.pallas_call(functools.partial(project_kernel, row_count, bits), out_sh...  93.5 us
    pallas_call x1, Pallas kernels, ending(): pl.pallas_call(functools.partial(ending_kernel, slabs), grid=(steps,), ou...  12.6 us
    add x2, other arithmetic, shards(): buffer_a, buffer_b = (MU * mom_a + grad_a, MU * mom_b + grad_b)  6.58 us

profile of v4, /device:TPU:0, one launch (start us, length us, event | category | flops | bytes accessed | tf_op | source)
XLA Modules:
  0.0 252.0 jit_solution(15336700088990333937)
XLA Ops:
  0.6 0.0 copy-start
  0.6 3.2 %multiply_add_fusion.1.refs_3_.refs_5_ = f32[896,384]{1,0:T(8,128)} fusion(f32[896,384]{1,0:T(8,128)} %param.10, f32[896,384]{1,0:T(8,128)} %param.9), kind=kLoop, calls=%fused_computation.1 | loop fusion | flops 688128 | bytes 4128768 | tf_op jit(solution)/shard_map/add | solution.py:948
  3.8 0.0 copy-done
  3.8 3.4 %multiply_add_fusion.refs_2_.refs_0_ = f32[192,3072]{1,0:T(8,128)} fusion(f32[192,3072]{1,0:T(8,128)S(1)} %copy-done, f32[192,3072]{1,0:T(8,128)} %param.6), kind=kLoop, calls=%fused_computation | loop fusion | flops 1179648 | bytes 7077888 | tf_op jit(solution)/shard_map/add | solution.py:948
  7.2 93.5 %project.1 = (f32[512,384]{1,0:T(8,128)}, f32[512,896]{1,0:T(8,128)}, f32[2,192,1536]{2,1,0:T(8,128)}) custom-call(f32[64,3072]{1,0:T(8,128)} %refs_0_.1, f32[64,384]{1,0:T(8,128)} %refs_1_.1, f32[192,3072]{1,0:T(8,128)} %multiply_add_fusion.refs_2_.refs_0_, f32[896,384]{1,0:T(8,128)} %multiply_add_fusion.1.refs_3_.refs_5_), custom_call_target="tpu_custom_call" | custom-call | tf_op jit(solution)/shard_map/project/pallas_call | solution.py:386
  100.8 137.9 %products.1 = (bf16[12,512,256]{2,1,0:T(8,128)(2,1)}, bf16[512,384]{1,0:T(8,128)(2,1)}, f32[12,64,256]{2,1,0:T(8,128)}, f32[64,384]{1,0:T(8,128)}, bf16[192,512]...) custom-call(f32[512,384]{1,0:T(8,128)} %get-tuple-element.22.refs_0_, ...), custom_call_target="tpu_custom_call" | custom-call | tf_op jit(solution)/shard_map/products/pallas_call | solution.py:851
  238.7 0.0 copy-start.1
  238.7 12.6 %ending.1 = (f32[192,3072]{1,0:T(8,128)}, bf16[192,3072]{1,0:T(8,128)(2,1)}, f32[64,3072]{1,0:T(8,128)}, f32[896,384]{1,0:T(8,128)}, bf16[896,384]{1,0:T(8,128)(2,1)}) custom-call(f32[192,3072]{1,0:T(8,128)} %multiply_add_fusion.refs_2_.refs_0_, bf16[12,512,256]{2,1,0:T(8,128)(2,1)} %get-tuple-element.25.refs_1_, f32[12,64,256]{2,1,0:T(8,128)} %get-tuple-element.26.refs_2_, ...), custom_call_target="tpu_custom_call" | custom-call | tf_op jit(solution)/shard_map/ending/pallas_call | solution.py:930
  251.3 0.0 copy-done.1
  251.3 0.6 copy.13
Async XLA Ops:
  0.6 3.2 %copy-start = (f32[192,3072]{1,0:T(8,128)S(1)}, f32[192,3072]{1,0:T(8,128)}, u32[]{:S(2)}) copy-start(f32[192,3072]{1,0:T(8,128)} %param.7) | copy-start | bytes 7077892
  238.7 12.6 %copy-start.1 = (f32[64,384]{1,0:T(8,128)S(1)}, f32[64,384]{1,0:T(8,128)}, u32[]{:S(2)}) copy-start(f32[64,384]{1,0:T(8,128)} %get-tuple-element.49) | copy-start | bytes 294916

commit v5 on v4

--- a/solution.py
+++ b/solution.py
@@ -638,12 +638,6 @@
     theirs_index = (1 - lane) * col_count + col
     cast_b[...] = dot(proj_b[rows_of(theirs_index, piece), :], proj_b[...], LAST)
     give_g().start()
-    piece_a[0][...] = dot(proj_a[rows_of(index, piece), :], proj_a[...], LAST)
-    gather(0, piece_a)
-    piece_b[0][...] = dot(proj_b[rows_of(index, piece), :], proj_b[...], LAST)
-    give_g().wait_recv()
-    piece_b[0][...] = piece_b[0][...] + land_b[...]
-    gather(1, piece_b)
     rows_high, rows_low = halves(proj_a[...])
 
     def multiply(k):
@@ -680,12 +674,24 @@
             take_v()
 
     early = jnp.logical_not(line.has_outer)
-    multiply(0)
-
-    @pl.when(early)
-    def _():
-        take(0)
-
+    piece_a[0][...] = dot(proj_a[rows_of(index, piece), :], proj_a[...], LAST)
+    gather(0, piece_a)
+
+    def produce(k):
+        multiply(k)
+
+        @pl.when(early)
+        def _():
+            take(k)
+
+    ahead = min(3, chunks)
+    produce(0)
+    piece_b[0][...] = dot(proj_b[rows_of(index, piece), :], proj_b[...], LAST)
+    give_g().wait_recv()
+    piece_b[0][...] = piece_b[0][...] + land_b[...]
+    gather(1, piece_b)
+    for k in range(1, ahead):
+        produce(k)
     for which, unit in enumerate((piece_a, piece_b)):
         spread(which, unit)
     gram_a[rows_of(index, piece), :] = piece_a[3][...]
@@ -693,32 +699,27 @@
     send_grams(0)
     whole_v[...] = split_dot(proj_b[...], buffer_b[...])
     give_v().start()
-    for k in range(1, chunks):
-        multiply(k)
-
-        @pl.when(early)
-        def _():
-            take(k)
-
-        if k == min(2, chunks - 1):
-
-            @pl.when(early)
-            def _():
-                take_v()
-
-            await_grams(0)
-            send_grams(1)
-        if k == min(3, chunks - 1):
-            later_take(0)
+    if ahead < chunks:
+        produce(ahead)
+    await_grams(0)
+    send_grams(1)
+
+    @pl.when(early)
+    def _():
+        take_v()
+
+    later_take(0)
+    for k in range(ahead + 1, chunks):
+        produce(k)
 
     tasks = []
     for k in range(chunks):
         if k > 0:
             tasks.append(functools.partial(later_take, k))
             tasks.append(functools.partial(hand, k - 1))
-        if k == min(2, chunks - 1):
+        if k == min(3, chunks - 1):
             tasks.append(later_take_v)
-        if k == min(3, chunks - 1):
+        if k == min(4, chunks - 1):
             tasks.append(hand_v)
     tasks.append(functools.partial(hand, chunks - 1))
     for stage in range(1, len(bits) + 1):
@@ -896,9 +897,13 @@
     buffer_a, trans_a, basis_a, ortho_a, scaled_a = refs[:5]
     buffer_b, trans_b, ortho_b, scaled_b = refs[5:9]
     mom_a, update_a, new_a, mom_b, update_b = refs[9:]
-    mom_a[...] = buffer_a[...] - (1.0 - MU) * narrow_dot(ortho_a[...], trans_a[0])
-    update_a[...] = narrow_dot(scaled_a[...], trans_a[0]).astype(jnp.bfloat16)
-    new_a[...] = basis_a[0]
+    width = trans_a.shape[2]
+    for k in range(trans_a.shape[0]):
+        columns = slice(k * width, (k + 1) * width)
+        change = narrow_dot(ortho_a[...], trans_a[k])
+        mom_a[:, columns] = buffer_a[:, columns] - (1.0 - MU) * change
+        update_a[:, columns] = narrow_dot(scaled_a[...], trans_a[k]).astype(jnp.bfloat16)
+        new_a[:, columns] = basis_a[k]
 
     @pl.when(pl.program_id(0) < slabs)
     def _():
@@ -909,8 +914,8 @@
 def ending(buffer_a, trans_a, basis_a, ortho_a, scaled_a, buffer_b, trans_b, ortho_b, scaled_b):
     steps, rank, width = trans_a.shape
     rows_a, rows_b, share = buffer_a.shape[0], buffer_b.shape[0], basis_a.shape[1]
-    slabs = 8
-    if width % 128 or rows_b % (16 * slabs) or steps < slabs:
+    slabs = 4
+    if width % 128 or rows_b % (16 * slabs) or steps % 2 or steps < 2 * slabs:
         flat = trans_a.swapaxes(0, 1).reshape(rank, -1)
         return (
             buffer_a - (1.0 - MU) * narrow_dot(ortho_a, flat),
@@ -920,16 +925,16 @@
             narrow_dot(scaled_b, trans_b).astype(jnp.bfloat16),
         )
     some = rows_b // slabs
-    cut = pl.BlockSpec((rows_a, width), lambda j: (0, j))
-    stack = pl.BlockSpec((1, rank, width), lambda j: (j, 0, 0))
-    thin = pl.BlockSpec((1, share, width), lambda j: (j, 0, 0))
+    cut = pl.BlockSpec((rows_a, 2 * width), lambda j: (0, j))
+    stack = pl.BlockSpec((2, rank, width), lambda j: (j, 0, 0))
+    thin = pl.BlockSpec((2, share, width), lambda j: (j, 0, 0))
     fixed_a = pl.BlockSpec((rows_a, rank), lambda j: (0, 0))
     fixed_b = pl.BlockSpec(trans_b.shape, lambda j: (0, 0))
     slab = pl.BlockSpec((some, buffer_b.shape[1]), lambda j: (jnp.minimum(j, slabs - 1), 0))
     rows = pl.BlockSpec((some, rank), lambda j: (jnp.minimum(j, slabs - 1), 0))
     return pl.pallas_call(
         functools.partial(ending_kernel, slabs),
-        grid=(steps,),
+        grid=(steps // 2,),
         out_shape=[
             jax.ShapeDtypeStruct(buffer_a.shape, jnp.float32),
             jax.ShapeDtypeStruct(buffer_a.shape, jnp.bfloat16),
@@ -938,7 +943,7 @@
             jax.ShapeDtypeStruct(buffer_b.shape, jnp.bfloat16),
         ],
         in_specs=[cut, stack, thin, fixed_a, fixed_a, slab, fixed_b, rows, rows],
-        out_specs=[cut, cut, pl.BlockSpec((share, width), lambda j: (0, j)), slab, slab],
+        out_specs=[cut, cut, pl.BlockSpec((share, 2 * width), lambda j: (0, j)), slab, slab],
         name="ending",
     )(buffer_a, trans_a, basis_a, ortho_a, scaled_a, buffer_b, trans_b, ortho_b, scaled_b)
 

time: 252 us -> 252 us (level)
    pallas_call x1, Pallas kernels: 12.6 us -> 9.61 us  [ending(): pl.pallas_call(functools.partial(ending_kernel, slabs), grid=(steps // 2,...]
    pallas_call x1, Pallas kernels: 138 us -> 141 us  [products(): pl.pallas_call(functools.partial(products_kernel, row_count, col_count, r...]
where the time goes in v5:
time: 252 us
  Pallas kernels  244 us (97%)
  other arithmetic  6.58 us (3%)
    pallas_call x1, Pallas kernels, products(): pl.pallas_call(functools.partial(products_kernel, row_count, col_count, r...  141 us
    pallas_call x1, Pallas kernels, project(): pl.pallas_call(functools.partial(project_kernel, row_count, bits), out_sh...  93.5 us
    pallas_call x1, Pallas kernels, ending(): pl.pallas_call(functools.partial(ending_kernel, slabs), grid=(steps // 2,...  9.61 us
    add x2, other arithmetic, shards(): buffer_a, buffer_b = (MU * mom_a + grad_a, MU * mom_b + grad_b)  6.58 us

profile of v5, /device:TPU:0, one launch (start us, length us, event | category | flops | bytes accessed | tf_op | source)
XLA Modules:
  0.0 251.8 jit_solution(15566110427758591061)
XLA Ops:
  0.6 0.0 copy-start
  0.6 3.2 %multiply_add_fusion.1.refs_3_.refs_5_ = f32[896,384]{1,0:T(8,128)} fusion(f32[896,384]{1,0:T(8,128)} %param.10, f32[896,384]{1,0:T(8,128)} %param.9), kind=kLoop, calls=%fused_computation.1 | loop fusion | flops 688128 | bytes 4128768 | tf_op jit(solution)/shard_map/add | solution.py:953
  3.8 0.0 copy-done
  3.8 3.4 %multiply_add_fusion.refs_2_.refs_0_ = f32[192,3072]{1,0:T(8,128)} fusion(f32[192,3072]{1,0:T(8,128)S(1)} %copy-done, f32[192,3072]{1,0:T(8,128)} %param.6), kind=kLoop, calls=%fused_computation | loop fusion | flops 1179648 | bytes 7077888 | tf_op jit(solution)/shard_map/add | solution.py:953
  7.2 93.5 %project.1 = (f32[512,384]{1,0:T(8,128)}, f32[512,896]{1,0:T(8,128)}, f32[2,192,1536]{2,1,0:T(8,128)}) custom-call(f32[64,3072]{1,0:T(8,128)} %refs_0_.1, f32[64,384]{1,0:T(8,128)} %refs_1_.1, f32[192,3072]{1,0:T(8,128)} %multiply_add_fusion.refs_2_.refs_0_, f32[896,384]{1,0:T(8,128)} %multiply_add_fusion.1.refs_3_.refs_5_), custom_call_target="tpu_custom_call" | custom-call | tf_op jit(solution)/shard_map/project/pallas_call | solution.py:386
  100.8 140.8 %products.1 = (bf16[12,512,256]{2,1,0:T(8,128)(2,1)}, bf16[512,384]{1,0:T(8,128)(2,1)}, f32[12,64,256]{2,1,0:T(8,128)}, f32[64,384]{1,0:T(8,128)}, bf16[192,512]...) custom-call(f32[512,384]{1,0:T(8,128)} %get-tuple-element.22.refs_0_, ...), custom_call_target="tpu_custom_call" | custom-call | tf_op jit(solution)/shard_map/products/pallas_call | solution.py:852
  241.6 0.0 copy-start.1
  241.6 9.6 %ending.1 = (f32[192,3072]{1,0:T(8,128)}, bf16[192,3072]{1,0:T(8,128)(2,1)}, f32[64,3072]{1,0:T(8,128)}, f32[896,384]{1,0:T(8,128)}, bf16[896,384]{1,0:T(8,128)(2,1)}) custom-call(f32[192,3072]{1,0:T(8,128)} %multiply_add_fusion.refs_2_.refs_0_, bf16[12,512,256]{2,1,0:T(8,128)(2,1)} %get-tuple-element.25.refs_1_, f32[12,64,256]{2,1,0:T(8,128)} %get-tuple-element.26.refs_2_, ...), custom_call_target="tpu_custom_call" | custom-call | tf_op jit(solution)/shard_map/ending/pallas_call | solution.py:935
  251.2 0.0 copy-done.1
  251.2 0.6 copy.13
Async XLA Ops:
  0.6 3.2 %copy-start = (f32[192,3072]{1,0:T(8,128)S(1)}, f32[192,3072]{1,0:T(8,128)}, u32[]{:S(2)}) copy-start(f32[192,3072]{1,0:T(8,128)} %param.7) | copy-start | bytes 7077892
  241.6 9.6 %copy-start.1 = (f32[64,384]{1,0:T(8,128)S(1)}, f32[64,384]{1,0:T(8,128)}, u32[]{:S(2)}) copy-start(f32[64,384]{1,0:T(8,128)} %get-tuple-element.49) | copy-start | bytes 294916

commit v6 on v4

--- a/solution.py
+++ b/solution.py
@@ -896,9 +896,13 @@
     buffer_a, trans_a, basis_a, ortho_a, scaled_a = refs[:5]
     buffer_b, trans_b, ortho_b, scaled_b = refs[5:9]
     mom_a, update_a, new_a, mom_b, update_b = refs[9:]
-    mom_a[...] = buffer_a[...] - (1.0 - MU) * narrow_dot(ortho_a[...], trans_a[0])
-    update_a[...] = narrow_dot(scaled_a[...], trans_a[0]).astype(jnp.bfloat16)
-    new_a[...] = basis_a[0]
+    width = trans_a.shape[2]
+    for k in range(trans_a.shape[0]):
+        columns = slice(k * width, (k + 1) * width)
+        change = narrow_dot(ortho_a[...], trans_a[k])
+        mom_a[:, columns] = buffer_a[:, columns] - (1.0 - MU) * change
+        update_a[:, columns] = narrow_dot(scaled_a[...], trans_a[k]).astype(jnp.bfloat16)
+        new_a[:, columns] = basis_a[k]
 
     @pl.when(pl.program_id(0) < slabs)
     def _():
@@ -909,8 +913,8 @@
 def ending(buffer_a, trans_a, basis_a, ortho_a, scaled_a, buffer_b, trans_b, ortho_b, scaled_b):
     steps, rank, width = trans_a.shape
     rows_a, rows_b, share = buffer_a.shape[0], buffer_b.shape[0], basis_a.shape[1]
-    slabs = 8
-    if width % 128 or rows_b % (16 * slabs) or steps < slabs:
+    slabs = 4
+    if width % 128 or rows_b % (16 * slabs) or steps % 2 or steps < 2 * slabs:
         flat = trans_a.swapaxes(0, 1).reshape(rank, -1)
         return (
             buffer_a - (1.0 - MU) * narrow_dot(ortho_a, flat),
@@ -920,16 +924,16 @@
             narrow_dot(scaled_b, trans_b).astype(jnp.bfloat16),
         )
     some = rows_b // slabs
-    cut = pl.BlockSpec((rows_a, width), lambda j: (0, j))
-    stack = pl.BlockSpec((1, rank, width), lambda j: (j, 0, 0))
-    thin = pl.BlockSpec((1, share, width), lambda j: (j, 0, 0))
+    cut = pl.BlockSpec((rows_a, 2 * width), lambda j: (0, j))
+    stack = pl.BlockSpec((2, rank, width), lambda j: (j, 0, 0))
+    thin = pl.BlockSpec((2, share, width), lambda j: (j, 0, 0))
     fixed_a = pl.BlockSpec((rows_a, rank), lambda j: (0, 0))
     fixed_b = pl.BlockSpec(trans_b.shape, lambda j: (0, 0))
     slab = pl.BlockSpec((some, buffer_b.shape[1]), lambda j: (jnp.minimum(j, slabs - 1), 0))
     rows = pl.BlockSpec((some, rank), lambda j: (jnp.minimum(j, slabs - 1), 0))
     return pl.pallas_call(
         functools.partial(ending_kernel, slabs),
-        grid=(steps,),
+        grid=(steps // 2,),
         out_shape=[
             jax.ShapeDtypeStruct(buffer_a.shape, jnp.float32),
             jax.ShapeDtypeStruct(buffer_a.shape, jnp.bfloat16),
@@ -938,7 +942,7 @@
             jax.ShapeDtypeStruct(buffer_b.shape, jnp.bfloat16),
         ],
         in_specs=[cut, stack, thin, fixed_a, fixed_a, slab, fixed_b, rows, rows],
-        out_specs=[cut, cut, pl.BlockSpec((share, width), lambda j: (0, j)), slab, slab],
+        out_specs=[cut, cut, pl.BlockSpec((share, 2 * width), lambda j: (0, j)), slab, slab],
         name="ending",
     )(buffer_a, trans_a, basis_a, ortho_a, scaled_a, buffer_b, trans_b, ortho_b, scaled_b)
 

time: 252 us -> 249 us (0.988)
  Pallas kernels: 244 us -> 241 us
    pallas_call x1, Pallas kernels: 12.6 us -> 9.58 us  [ending(): pl.pallas_call(functools.partial(ending_kernel, slabs), grid=(steps // 2,...]
where the time goes in v6:
time: 249 us
  Pallas kernels  241 us (97%)
  other arithmetic  6.58 us (3%)
    pallas_call x1, Pallas kernels, products(): pl.pallas_call(functools.partial(products_kernel, row_count, col_count, r...  138 us
    pallas_call x1, Pallas kernels, project(): pl.pallas_call(functools.partial(project_kernel, row_count, bits), out_sh...  93.5 us
    pallas_call x1, Pallas kernels, ending(): pl.pallas_call(functools.partial(ending_kernel, slabs), grid=(steps // 2,...  9.58 us
    add x2, other arithmetic, shards(): buffer_a, buffer_b = (MU * mom_a + grad_a, MU * mom_b + grad_b)  6.58 us

profile of v6, /device:TPU:0, one launch (start us, length us, event | category | flops | bytes accessed | tf_op | source)
XLA Modules:
  0.0 248.9 jit_solution(2787600571186062412)
XLA Ops:
  0.6 0.0 copy-start
  0.6 3.2 %multiply_add_fusion.1.refs_3_.refs_5_ = f32[896,384]{1,0:T(8,128)} fusion(f32[896,384]{1,0:T(8,128)} %param.10, f32[896,384]{1,0:T(8,128)} %param.9), kind=kLoop, calls=%fused_computation.1 | loop fusion | flops 688128 | bytes 4128768 | tf_op jit(solution)/shard_map/add | solution.py:952
  3.8 0.0 copy-done
  3.8 3.4 %multiply_add_fusion.refs_2_.refs_0_ = f32[192,3072]{1,0:T(8,128)} fusion(f32[192,3072]{1,0:T(8,128)S(1)} %copy-done, f32[192,3072]{1,0:T(8,128)} %param.6), kind=kLoop, calls=%fused_computation | loop fusion | flops 1179648 | bytes 7077888 | tf_op jit(solution)/shard_map/add | solution.py:952
  7.2 93.5 %project.1 = (f32[512,384]{1,0:T(8,128)}, f32[512,896]{1,0:T(8,128)}, f32[2,192,1536]{2,1,0:T(8,128)}) custom-call(f32[64,3072]{1,0:T(8,128)} %refs_0_.1, f32[64,384]{1,0:T(8,128)} %refs_1_.1, f32[192,3072]{1,0:T(8,128)} %multiply_add_fusion.refs_2_.refs_0_, f32[896,384]{1,0:T(8,128)} %multiply_add_fusion.1.refs_3_.refs_5_), custom_call_target="tpu_custom_call" | custom-call | tf_op jit(solution)/shard_map/project/pallas_call | solution.py:386
  100.8 137.9 %products.1 = (bf16[12,512,256]{2,1,0:T(8,128)(2,1)}, bf16[512,384]{1,0:T(8,128)(2,1)}, f32[12,64,256]{2,1,0:T(8,128)}, f32[64,384]{1,0:T(8,128)}, bf16[192,512]...) custom-call(f32[512,384]{1,0:T(8,128)} %get-tuple-element.22.refs_0_, ...), custom_call_target="tpu_custom_call" | custom-call | tf_op jit(solution)/shard_map/products/pallas_call | solution.py:851
  238.7 0.0 copy-start.1
  238.7 9.6 %ending.1 = (f32[192,3072]{1,0:T(8,128)}, bf16[192,3072]{1,0:T(8,128)(2,1)}, f32[64,3072]{1,0:T(8,128)}, f32[896,384]{1,0:T(8,128)}, bf16[896,384]{1,0:T(8,128)(2,1)}) custom-call(f32[192,3072]{1,0:T(8,128)} %multiply_add_fusion.refs_2_.refs_0_, bf16[12,512,256]{2,1,0:T(8,128)(2,1)} %get-tuple-element.25.refs_1_, f32[12,64,256]{2,1,0:T(8,128)} %get-tuple-element.26.refs_2_, ...), custom_call_target="tpu_custom_call" | custom-call | tf_op jit(solution)/shard_map/ending/pallas_call | solution.py:934
  248.3 0.0 copy-done.1
  248.3 0.6 copy.13
Async XLA Ops:
  0.6 3.2 %copy-start = (f32[192,3072]{1,0:T(8,128)S(1)}, f32[192,3072]{1,0:T(8,128)}, u32[]{:S(2)}) copy-start(f32[192,3072]{1,0:T(8,128)} %param.7) | copy-start | bytes 7077892
  238.7 9.6 %copy-start.1 = (f32[64,384]{1,0:T(8,128)S(1)}, f32[64,384]{1,0:T(8,128)}, u32[]{:S(2)}) copy-start(f32[64,384]{1,0:T(8,128)} %get-tuple-element.49) | copy-start | bytes 294916
